TPU v7x, 32 devices: a whole 2x2x4 slice. The times are simulated.
32 devices in a mesh: mode: 2 (over y), col: 16 (over z, x, core).
Axes of the slice: x: 2, y: 2, z: 4, core: 2. Of those that a mesh axis runs over, the one named last changes fastest.
Arguments:
- tensor: float32 [512, 16, 4096], P('mode', 'col'), may hold values from -15 to 15
- start_basis: float32 [512, 128], replicated, may hold values from -6 to 6
Outputs:
- factor: float32 [512, 512], replicated
- basis: float32 [512, 128], replicated
- core: float32 [128, 16, 4096], P(None, 'col', 'mode')
All inputs are finite; a program needn't handle non-finite values.
Results may differ from a plain program's by a relative error of at most 0.00018.
Values sent between devices are 32-bit elements; how exact they have to be, the bound alone decides.
A program may use at most 64 MiB of HBM per device.

v0:
```python
import functools

import jax
import jax.numpy as jnp
from jax import lax
from jax.experimental import pallas as pl
from jax.experimental.pallas import tpu as pltpu
from jax.sharding import PartitionSpec as P

POWER = 2
BLOCK = 128
PANEL = 8
CHUNK = 512
MESH = pl.DeviceIdType.MESH


def halves(value):
    high = value.astype(jnp.bfloat16)
    low = (value - high.astype(jnp.float32)).astype(jnp.bfloat16)
    return high, low


def contract(left, right, dims):
    return lax.dot_general(left, right, (dims, ((), ())), preferred_element_type=jnp.float32)


def exact(left, right, dims):
    return lax.dot_general(
        left, right, (dims, ((), ())), precision=lax.Precision.HIGHEST,
        preferred_element_type=jnp.float32,
    )


NN = ((1,), (0,))
NT = ((1,), (1,))
TN = ((0,), (0,))


def split3(value):
    high = value.astype(jnp.bfloat16).astype(jnp.float32)
    rest = value - high
    middle = rest.astype(jnp.bfloat16).astype(jnp.float32)
    return high, middle, rest - middle


def eliminate_panel(aug, j):
    size, width = aug.shape
    first = PANEL * j
    rows = [aug[first + t : first + t + 1, :] for t in range(PANEL)]
    entry = {}
    for t in range(PANEL):
        for s in range(t, PANEL):
            value = rows[t][:, first + s : first + s + 1]
            entry[s, t] = jnp.broadcast_to(value, (1, size))
    pivots = []
    for t in range(PANEL):
        pivot = entry[t, t]
        pivots.append(pivot)
        inverse = 1.0 / pivot
        for s in range(t + 1, PANEL):
            ratio = entry[s, t] * inverse
            for u in range(s, PANEL):
                entry[u, s] = entry[u, s] - ratio * entry[u, t]
            rows[s] = rows[s] - jnp.concatenate([ratio] * (width // size), axis=1) * rows[t]
    done = []
    for t in range(PANEL):
        scale = lax.rsqrt(pivots[t])
        done.append(rows[t] * jnp.concatenate([scale] * (width // size), axis=1))
    panel = jnp.concatenate(done, axis=0)
    aug[first : first + PANEL, :] = panel
    below = first + PANEL
    if below < size:
        high, middle, low = split3(panel)
        left = jnp.concatenate([high, high, middle, high, low, middle], axis=0).astype(jnp.bfloat16)
        right = jnp.concatenate([high, middle, high, low, high, middle], axis=0).astype(jnp.bfloat16)
        aug[below:size, :] = aug[below:size, :] - contract(left[:, below:size], right, TN)


def eliminate(augs):
    for j in range(BLOCK // PANEL):
        for aug in augs:
            eliminate_panel(aug, j)


def load_augmented(aug, matrix):
    size = matrix.shape[0]
    row = lax.broadcasted_iota(jnp.int32, (size, size), 0)
    column = lax.broadcasted_iota(jnp.int32, (size, size), 1)
    aug[:, 0:size] = matrix
    aug[:, size : 2 * size] = jnp.where(row == column, 1.0, 0.0).astype(jnp.float32)


def lower_blocks(blocks):
    return [(i, k) for i in range(blocks) for k in range(i + 1)]


def stages_of(modes, cols):
    stages, stride = [], 1
    first = 2 if cols % 2 == 0 else 1
    if first > 1:
        stages.append((1, first, False))
        stride = first
    second = 2 if (cols // stride) % 2 == 0 else 1
    stages.append((stride, second, True))
    stride *= second
    if cols // stride > 1:
        stages.append((stride, cols // stride, False))
    return stages


def round_up(value, unit):
    return -(-value // unit) * unit


def layout_of(size, modes, cols):
    pairs = lower_blocks(size // BLOCK)
    rows = size // modes
    inner = []
    if rows % BLOCK == 0 and modes > 1:
        inner = lower_blocks(rows // BLOCK)
    per = rows // BLOCK
    extent = round_up(len(inner) * BLOCK, 8 * cols)
    where = {}
    for m in range(modes):
        for n, (i, k) in enumerate(inner):
            where[m * per + i, m * per + k] = m * extent + n * BLOCK
    outer = [pair for pair in pairs if pair not in where]
    for n, pair in enumerate(outer):
        where[pair] = modes * extent + n * BLOCK
    return where, inner, extent, outer, round_up(len(outer) * BLOCK, 8 * modes * cols)


def members_of(stages, modes):
    return [count * (modes if with_mode else 1) for _, count, with_mode in stages]


def gather_kernel(modes, cols, x_ref, flat_ref, total_ref, local, acc_in, acc_out, main, cross, *rest):
    mode, col = lax.axis_index("mode"), lax.axis_index("col")
    all_stages = stages_of(modes, cols)
    col_stages = [(stride, count, False) for stride, count, _ in all_stages]
    n = len(all_stages)
    slots_in, slots_out = rest[:n], rest[n : 2 * n]
    local_sem, piece_send, piece_recv, swap_send, swap_recv, in_sems, out_sems, share_in, share_out = rest[2 * n :]
    rows, depth, length = x_ref.shape
    size = rows * modes
    width = length // modes
    chunk = min(CHUNK, width)
    per = width // chunk
    chunks = depth * per
    where, inner, in_extent, outer, out_extent = layout_of(size, modes, cols)

    def position(stage):
        stride, count, with_mode = stage
        place = lax.rem(lax.div(col, stride), count)
        return place * modes + mode if with_mode else place

    def members(stage):
        return stage[1] * (modes if stage[2] else 1)

    def peer(stage, offset):
        stride, count, with_mode = stage
        other = lax.rem(position(stage) + offset, members(stage))
        place = lax.div(other, modes) if with_mode else other
        there = col + (place - lax.rem(lax.div(col, stride), count)) * stride
        return other, (lax.rem(other, modes) if with_mode else mode, there)

    partners = [(lax.rem(mode + d, modes), col) for d in range(1, modes)]
    greeted = []
    for stage in all_stages:
        greeted += [peer(stage, d)[1] for d in range(1, members(stage))]
    barrier = pltpu.get_barrier_semaphore()
    for device in greeted:
        pl.semaphore_signal(barrier, inc=1, device_id=device, device_id_type=MESH)
    pl.semaphore_wait(barrier, len(greeted))

    own_rows = pl.ds(pl.multiple_of(mode * rows, rows), rows)

    def spans(c):
        layer, part = lax.div(c, per), lax.rem(c, per)
        return layer, part * chunk, pl.multiple_of(layer * width + part * chunk, chunk)

    def piece(c, d):
        layer, start, target = spans(c)
        source = pl.multiple_of(lax.rem(mode + d, modes) * width + start, chunk)
        return pltpu.make_async_remote_copy(
            src_ref=x_ref.at[:, layer, pl.ds(source, chunk)],
            dst_ref=flat_ref.at[own_rows, pl.ds(target, chunk)],
            send_sem=piece_send.at[d - 1, c],
            recv_sem=piece_recv.at[d - 1, c],
            device_id=partners[d - 1],
            device_id_type=MESH,
        )

    def load(c):
        layer, part = lax.div(c, per * modes), lax.rem(c, per * modes)
        source = pl.multiple_of(part * chunk, chunk)
        target = pl.multiple_of(layer * length + part * chunk, chunk)
        return pltpu.make_async_copy(
            x_ref.at[:, layer, pl.ds(source, chunk)], local.at[:, pl.ds(target, chunk)], local_sem.at[c]
        ), target

    def begin(c, carry):
        for d in range(1, modes):
            piece(c, d).start()
        return carry

    def begin_load(c, carry):
        load(c)[0].start()
        return carry

    early = max(chunks // 2, 1)
    lax.fori_loop(0, early, begin, 0)
    lax.fori_loop(0, chunks * modes, begin_load, 0)

    main[...] = jnp.zeros_like(main)
    cross[...] = jnp.zeros_like(cross)

    def accumulate_in(c, carry):
        copy, target = load(c)
        copy.wait()
        if inner:
            high, low = halves(local[:, pl.ds(target, chunk)])
            main[0:rows, 0:rows] += contract(high, high, NT)
            cross[0:rows, 0:rows] += contract(high, low, NT)
        return carry

    lax.fori_loop(0, chunks * modes, accumulate_in, 0)
    for layer in range(depth):
        source = pl.multiple_of(layer * length + mode * width, chunk)
        flat_ref[own_rows, layer * width : (layer + 1) * width] = local[:, pl.ds(source, width)]

    def pack(acc, pairs, extent):
        for at, (i, k) in enumerate(pairs):
            tall, wide = slice(i * BLOCK, (i + 1) * BLOCK), slice(k * BLOCK, (k + 1) * BLOCK)
            acc[at * BLOCK : (at + 1) * BLOCK, :] = main[tall, wide] + (cross[tall, wide] + cross[wide, tall].T)
        used = len(pairs) * BLOCK
        if used < extent:
            acc[used:, :] = jnp.zeros((extent - used, BLOCK), jnp.float32)

    def scatter_sum(stages, acc, extent, slots, sems, target):
        base, bases = 0, []
        for g, stage in enumerate(stages):
            count = members(stage)
            part = extent // count
            copies = []
            for d in range(1, count):
                other, device = peer(stage, d)
                copy = pltpu.make_async_remote_copy(
                    src_ref=acc.at[pl.ds(pl.multiple_of(base + other * part, 8), part), :],
                    dst_ref=slots[g].at[d - 1],
                    send_sem=sems.at[0, g, d - 1],
                    recv_sem=sems.at[1, g, d - 1],
                    device_id=device,
                    device_id_type=MESH,
                )
                copy.start()
                copies.append(copy)
            base = base + position(stage) * part
            extent = part
            bases.append((base, part))
            for copy in copies:
                copy.wait()
            mine = pl.ds(pl.multiple_of(base, 8), part)
            added = acc[mine, :]
            for d in range(1, count):
                added = added + slots[g][d - 1]
            if g < len(stages) - 1:
                acc[mine, :] = added
            else:
                total_ref[pl.ds(pl.multiple_of(target + base, 8), part), :] = added
        return bases

    def share(stages, bases, targets, sems):
        for g in reversed(range(len(stages))):
            stage = stages[g]
            base, part = bases[g]
            copies = []
            for d in range(1, members(stage)):
                for t, target in enumerate(targets):
                    mine = pl.ds(pl.multiple_of(target + base, 8), part)
                    copy = pltpu.make_async_remote_copy(
                        src_ref=total_ref.at[mine, :],
                        dst_ref=total_ref.at[mine, :],
                        send_sem=sems.at[0, g, (d - 1) * len(targets) + t],
                        recv_sem=sems.at[1, g, (d - 1) * len(targets) + t],
                        device_id=peer(stage, d)[1],
                        device_id_type=MESH,
                    )
                    copy.start()
                    copies.append(copy)
            for copy in copies:
                copy.wait()

    def accumulate_out(c, carry):
        for d in range(1, modes):
            piece(c, d).wait_recv()
        high, low = halves(flat_ref[:, pl.ds(spans(c)[2], chunk)])
        if inner:
            for m in range(1, modes):
                tall, wide = slice(m * rows, (m + 1) * rows), slice(0, m * rows)
                main[tall, wide] += contract(high[tall, :], high[wide, :], NT) + contract(low[tall, :], high[wide, :], NT)
                cross[tall, wide] += contract(high[tall, :], low[wide, :], NT)
        else:
            main[...] += contract(high, high, NT)
            cross[...] += contract(high, low, NT)
        return carry

    swaps = []
    if inner:
        pack(acc_in, inner, in_extent)
        main[...] = jnp.zeros_like(main)
        cross[...] = jnp.zeros_like(cross)
        bases = scatter_sum(col_stages, acc_in, in_extent, slots_in, in_sems, mode * in_extent)
        base, part = bases[-1]
        mine = pl.ds(pl.multiple_of(mode * in_extent + base, 8), part)
        for d in range(1, modes):
            swap = pltpu.make_async_remote_copy(
                src_ref=total_ref.at[mine, :],
                dst_ref=total_ref.at[mine, :],
                send_sem=swap_send.at[d - 1],
                recv_sem=swap_recv.at[d - 1],
                device_id=partners[d - 1],
                device_id_type=MESH,
            )
            swap.start()
            swaps.append(swap)
    lax.fori_loop(early, chunks, begin, 0)
    lax.fori_loop(0, early, accumulate_out, 0)
    if inner:
        for swap in swaps:
            swap.wait()
        share(col_stages, bases, [m * in_extent for m in range(modes)], share_in)
    lax.fori_loop(early, chunks, accumulate_out, 0)

    pack(acc_out, outer, out_extent)
    bases = scatter_sum(all_stages, acc_out, out_extent, slots_out, out_sems, modes * in_extent)
    share(all_stages, bases, [modes * in_extent], share_out)

    def end(c, carry):
        for d in range(1, modes):
            piece(c, d).wait_send()
        return carry

    lax.fori_loop(0, chunks, end, 0)


def gather(tensor):
    modes, cols = lax.axis_size("mode"), lax.axis_size("col")
    rows, depth, length = tensor.shape
    size = rows * modes
    width = length // modes
    chunks = depth * (width // min(CHUNK, width))
    stages = stages_of(modes, cols)
    _, inner, in_extent, _, out_extent = layout_of(size, modes, cols)
    in_extent = max(in_extent, 8 * cols)
    slots_in, slots_out, extent_in, extent, most = [], [], in_extent, out_extent, 1
    for stride, count, with_mode in stages:
        extent_in = extent_in // count
        slots_in.append(pltpu.VMEM((max(count - 1, 1), extent_in, BLOCK), jnp.float32))
        count = count * (modes if with_mode else 1)
        extent = extent // count
        slots_out.append(pltpu.VMEM((max(count - 1, 1), extent, BLOCK), jnp.float32))
        most = max(most, count - 1)
    dma = pltpu.SemaphoreType.DMA
    vmem = pl.BlockSpec(memory_space=pltpu.VMEM)
    packed = (modes * in_extent if inner else 0) + out_extent
    return pl.pallas_call(
        functools.partial(gather_kernel, modes, cols),
        out_shape=(
            jax.ShapeDtypeStruct((size, depth * width), jnp.float32),
            jax.ShapeDtypeStruct((packed, BLOCK), jnp.float32),
        ),
        in_specs=[pl.BlockSpec(memory_space=pl.ANY)],
        out_specs=(vmem, vmem),
        scratch_shapes=[
            pltpu.VMEM((rows, depth * length), jnp.float32),
            pltpu.VMEM((in_extent, BLOCK), jnp.float32),
            pltpu.VMEM((out_extent, BLOCK), jnp.float32),
            pltpu.VMEM((size, size), jnp.float32),
            pltpu.VMEM((size, size), jnp.float32),
            *slots_in,
            *slots_out,
            dma((chunks * modes,)),
            *[dma((max(modes - 1, 1), chunks))] * 2,
            *[dma((max(modes - 1, 1),))] * 2,
            *[dma((2, len(stages), most))] * 2,
            dma((2, len(stages), most * modes)),
            dma((2, len(stages), most)),
        ],
        compiler_params=pltpu.CompilerParams(collective_id=0, has_side_effects=True),
        name="gather",
    )(tensor)


def linear_kernel(columns, where, packed_ref, start_ref, flat_ref, factor_ref, basis_ref, core_ref, gram, work, image, aug_f, aug_b, core, core_sem):
    size, rank = start_ref.shape
    blocks = size // BLOCK
    row = lax.broadcasted_iota(jnp.int32, (BLOCK, BLOCK), 0)
    column = lax.broadcasted_iota(jnp.int32, (BLOCK, BLOCK), 1)
    scale = 1.0 / columns
    for (i, k), at in where.items():
        scaled = packed_ref[at : at + BLOCK, :] * scale
        gram[i * BLOCK : (i + 1) * BLOCK, k * BLOCK : (k + 1) * BLOCK] = scaled
        work[i * BLOCK : (i + 1) * BLOCK, k * BLOCK : (k + 1) * BLOCK] = scaled
        if i != k:
            gram[k * BLOCK : (k + 1) * BLOCK, i * BLOCK : (i + 1) * BLOCK] = scaled.T

    for step in range(max(blocks, POWER)):
        augs = []
        if step < blocks:
            at = step * BLOCK
            load_augmented(aug_f, work[at : at + BLOCK, at : at + BLOCK])
            augs.append(aug_f)
        if step < POWER:
            source = start_ref if step == 0 else basis_ref
            image[...] = exact(gram[...], source[...], NN)
            load_augmented(aug_b, exact(image[...], image[...], TN))
            augs.append(aug_b)
        eliminate(augs)
        if step < POWER:
            basis_ref[...] = exact(image[...], aug_b[:, rank : 2 * rank], NT)
        if step < blocks:
            upper = jnp.where(row <= column, aug_f[:, 0:BLOCK], 0.0)
            factor_ref[at : at + BLOCK, at : at + BLOCK] = upper.T
            if step > 0:
                factor_ref[0:at, at : at + BLOCK] = jnp.zeros((at, BLOCK), jnp.float32)
            below = at + BLOCK
            if below < size:
                inverse = aug_f[:, BLOCK : 2 * BLOCK]
                left = exact(work[below:size, at : at + BLOCK], inverse, NT)
                factor_ref[below:size, at : at + BLOCK] = left
                work[below:size, below:size] = work[below:size, below:size] - exact(left, left, NT)

    high, low = halves(basis_ref[...])
    depth, length = core_ref.shape[1:]
    width = min(CHUNK, length)
    copies = []
    for start in range(0, depth * length, width):
        part = slice(start, start + width)
        flat_high, flat_low = halves(flat_ref[:, part])
        core[:, part] = contract(high, flat_high, TN) + contract(high, flat_low, TN) + contract(low, flat_high, TN)
        layer, offset = divmod(start, length)
        copy = pltpu.make_async_copy(
            core.at[:, part], core_ref.at[:, layer, offset : offset + width], core_sem.at[len(copies)]
        )
        copy.start()
        copies.append(copy)
    for copy in copies:
        copy.wait()


def linear(columns, depth, packed, start_basis, flat):
    size, rank = start_basis.shape
    length = flat.shape[1] // depth
    where = layout_of(size, lax.axis_size("mode"), lax.axis_size("col"))[0]
    vmem = pl.BlockSpec(memory_space=pltpu.VMEM)
    return pl.pallas_call(
        functools.partial(linear_kernel, columns, where),
        out_shape=(
            jax.ShapeDtypeStruct((size, size), jnp.float32),
            jax.ShapeDtypeStruct((size, rank), jnp.float32),
            jax.ShapeDtypeStruct((rank, depth, length), jnp.float32),
        ),
        in_specs=[vmem] * 3,
        out_specs=(vmem, vmem, pl.BlockSpec(memory_space=pl.ANY)),
        scratch_shapes=[
            pltpu.VMEM((size, size), jnp.float32),
            pltpu.VMEM((size, size), jnp.float32),
            pltpu.VMEM((size, rank), jnp.float32),
            pltpu.VMEM((BLOCK, 2 * BLOCK), jnp.float32),
            pltpu.VMEM((rank, 2 * rank), jnp.float32),
            pltpu.VMEM((rank, flat.shape[1]), jnp.float32),
            pltpu.SemaphoreType.DMA((flat.shape[1] // min(CHUNK, length),)),
        ],
        name="linear",
    )(packed, start_basis, flat)


def per_device(tensor, start_basis):
    depth = tensor.shape[1]
    flat, packed = gather(tensor)
    columns = flat.shape[1] * lax.axis_size("mode") * lax.axis_size("col")
    factor, basis, core = linear(columns, depth, packed, start_basis, flat)
    return (factor, basis, core)


def solution(mesh):
    in_specs = (P("mode", "col", None), P())
    out_specs = (P(), P(), P(None, "col", "mode"))
    return jax.shard_map(
        per_device, mesh=mesh, in_specs=in_specs, out_specs=out_specs, check_vma=False
    )
```

profile of v0, /device:TPU:0, one launch (start us, length us, event | category | flops | bytes accessed | tf_op | source)
XLA Modules:
  0.0 112.6 jit_solution(11883949148700334848)
XLA Ops:
  0.6 73.3 %gather.1 = (f32[512,2048]{1,0:T(8,128)}, f32[1280,128]{1,0:T(8,128)}) custom-call(f32[256,1,4096]{2,1,0:T(1,128)} %x_ref.1), custom_call_target="tpu_custom_call" | custom-call | tf_op jit(solution)/shard_map/gather/pallas_call | solution.py:367
  73.9 38.5 %linear.1 = (f32[512,512]{1,0:T(8,128)}, f32[512,128]{1,0:T(8,128)}, f32[128,1,2048]{2,1,0:T(1,128)}) custom-call(f32[1280,128]{1,0:T(8,128)} %get-tuple-element.5.packed_ref, f32[512,128]{1,0:T(8,128)} %start_ref.1, f32[512,2048]{1,0:T(8,128)} %get-tuple-element.6.flat_ref), custom_call_target="tpu_custom_call" | custom-call | tf_op jit(solution)/shard_map/linear/pallas_call | solution.py:457
where the time goes:
time: 113 us
  Pallas kernels  112 us (99%)
    pallas_call x1, Pallas kernels, gather(): pl.pallas_call(functools.partial(gather_kernel, modes, cols), out_shape=(...  73.3 us
    pallas_call x1, Pallas kernels, linear(): pl.pallas_call(functools.partial(linear_kernel, columns, where), out_shap...  38.5 us

commit v1 on v0

--- a/solution.py
+++ b/solution.py
@@ -476,12 +476,416 @@
     )(packed, start_basis, flat)
 
 
+def fast_case(modes, cols, shape):
+    rows, depth, length = shape
+    return modes == 2 and depth == 1 and rows % (2 * BLOCK) == 0 and cols % 2 == 0 and cols > 2 and length % (2 * BLOCK) == 0
+
+
+STRIPS = 8
+LATE = 2
+EARLY = 3
+SEMAPHORES = 240
+
+
+def fast_layout(rows, cols):
+    per = rows // BLOCK
+    strip = rows // STRIPS
+    first = rows - LATE * strip
+    inner = lower_blocks(per)
+    unit = 8 * cols
+    extents = [round_up(len(inner) * BLOCK, unit), round_up(first * per, unit), round_up((rows - first) * per, unit)]
+    starts, at = [], 0
+    for extent in extents:
+        starts.append(at)
+        at += 2 * extent
+    return per, strip, first, inner, extents, starts, at
+
+
+def fast_gather_kernel(cols, columns, x_ref, recv_out, total_ref, lead_ref, inverse_ref, local, recv, own_high, own_low, main, cross, work, aug, acc_in, acc_a, acc_b, *rest):
+    slots, sems = rest[:-1], rest[-1]
+    mode, col = lax.axis_index("mode"), lax.axis_index("col")
+    other_mode = 1 - mode
+    rows, _, length = x_ref.shape
+    width = length // 2
+    chips = cols // 2
+    per, strip, first, inner, extents, starts, _ = fast_layout(rows, cols)
+    core, chip = lax.rem(col, 2), lax.div(col, 2)
+    counter = [0]
+    pending = []
+
+    def sem():
+        counter[0] += 1
+        return sems.at[counter[0] - 1]
+
+    def push(source, target, device):
+        copy = pltpu.make_async_remote_copy(
+            src_ref=source, dst_ref=target, send_sem=sem(), recv_sem=sem(), device_id=device, device_id_type=MESH
+        )
+        copy.start()
+        pending.append(copy)
+        return copy
+
+    sibling = (mode, chip * 2 + 1 - core)
+    partner = (other_mode, col)
+    plane = []
+    for d in range(1, chips):
+        place = lax.rem(chip + d, chips)
+        plane.append((place, (mode, place * 2 + core)))
+    across = [(other_mode, lax.rem(chip + d, chips) * 2 + core) for d in range(chips)]
+
+    greeted = [sibling] + [device for _, device in plane] + across
+    barrier = pltpu.get_barrier_semaphore()
+    for device in greeted:
+        pl.semaphore_signal(barrier, inc=1, device_id=device, device_id_type=MESH)
+    pl.semaphore_wait(barrier, len(greeted))
+
+    pieces = []
+    away = pl.ds(pl.multiple_of(other_mode * width, width), width)
+
+    def send_piece(k):
+        span = slice(k * strip, (k + 1) * strip)
+        pieces.append(push(x_ref.at[span, 0, away], recv.at[span, :], partner))
+
+    for k in range(EARLY):
+        send_piece(k)
+
+    loads = []
+    part = length // 4
+    for c in range(4):
+        span = slice(c * part, (c + 1) * part)
+        copy = pltpu.make_async_copy(x_ref.at[:, 0, span], local.at[:, span], sem())
+        copy.start()
+        loads.append(copy)
+    for c in range(4):
+        loads[c].wait()
+        high, low = halves(local[:, c * part : (c + 1) * part])
+        if c == 0:
+            main[...] = contract(high, high, NT)
+            cross[...] = contract(high, low, NT)
+        else:
+            main[...] += contract(high, high, NT)
+            cross[...] += contract(high, low, NT)
+
+    for at, (i, k) in enumerate(inner):
+        tall, wide = slice(i * BLOCK, (i + 1) * BLOCK), slice(k * BLOCK, (k + 1) * BLOCK)
+        acc_in[at * BLOCK : (at + 1) * BLOCK, :] = main[tall, wide] + (cross[tall, wide] + cross[wide, tall].T)
+
+    def fill(acc, used):
+        if used < acc.shape[0]:
+            acc[used:, :] = jnp.zeros((acc.shape[0] - used, BLOCK), jnp.float32)
+
+    def rows_at(base, count):
+        return pl.ds(pl.multiple_of(base, 8), count)
+
+    def core_send(acc, slot):
+        half = acc.shape[0] // 2
+        return push(acc.at[rows_at((1 - core) * half, half), :], slot.at[...], sibling)
+
+    def core_add(acc, slot, copy):
+        half = acc.shape[0] // 2
+        copy.wait_recv()
+        mine = rows_at(core * half, half)
+        acc[mine, :] = acc[mine, :] + slot[...]
+
+    def plane_send(acc, slot):
+        half = acc.shape[0] // 2
+        share = half // chips
+        copies = []
+        for d, (place, device) in enumerate(plane):
+            copies.append(push(acc.at[rows_at(core * half + place * share, share), :], slot.at[d], device))
+        return copies
+
+    def plane_add(acc, slot, copies, start):
+        half = acc.shape[0] // 2
+        share = half // chips
+        base = core * half + chip * share
+        for copy in copies:
+            copy.wait_recv()
+        added = acc[rows_at(base, share), :]
+        for d in range(chips - 1):
+            added = added + slot[d]
+        total_ref[rows_at(start + mode * acc.shape[0] + base, share), :] = added
+
+    def swap(acc, start):
+        half = acc.shape[0] // 2
+        share = half // chips
+        mine = rows_at(start + mode * acc.shape[0] + core * half + chip * share, share)
+        return push(total_ref.at[mine, :], total_ref.at[mine, :], partner)
+
+    def plane_share(acc, start):
+        half = acc.shape[0] // 2
+        share = half // chips
+        copies = []
+        for _, device in plane:
+            for m in range(2):
+                mine = rows_at(start + m * acc.shape[0] + core * half + chip * share, share)
+                copies.append(push(total_ref.at[mine, :], total_ref.at[mine, :], device))
+        return copies
+
+    def direct_share(acc, start):
+        half = acc.shape[0] // 2
+        share = half // chips
+        mine = rows_at(start + mode * acc.shape[0] + core * half + chip * share, share)
+        devices = [device for _, device in plane] + across
+        return [push(total_ref.at[mine, :], total_ref.at[mine, :], device) for device in devices]
+
+    def core_share(acc, start):
+        half = acc.shape[0] // 2
+        copies = []
+        for m in range(2):
+            mine = rows_at(start + m * acc.shape[0] + core * half, half)
+            copies.append(push(total_ref.at[mine, :], total_ref.at[mine, :], sibling))
+        return copies
+
+    def arrive(copies):
+        for copy in copies:
+            copy.wait_recv()
+
+    outgoing = []
+
+    def strips(begin, end, acc, offset, tall):
+        arrive(pieces[begin:end])
+        span = slice(begin * strip, end * strip)
+        copy = pltpu.make_async_copy(recv.at[span, :], recv_out.at[span, :], sem())
+        copy.start()
+        outgoing.append(copy)
+        high, low = halves(recv[span, :])
+        value = contract(high, own_high[...], NT) + (contract(high, own_low[...], NT) + contract(low, own_high[...], NT))
+        for c in range(per):
+            at = c * tall + begin * strip - offset
+            acc[at : at + (end - begin) * strip, :] = value[:, c * BLOCK : (c + 1) * BLOCK]
+
+    fill(acc_in, len(inner) * BLOCK)
+    copy = core_send(acc_in, slots[0])
+    mine = local[:, pl.ds(pl.multiple_of(mode * width, width), width)]
+    high, low = halves(mine)
+    own_high[...] = high
+    own_low[...] = low
+    core_add(acc_in, slots[0], copy)
+    copies = plane_send(acc_in, slots[1])
+    plane_add(acc_in, slots[1], copies, starts[0])
+    copy = swap(acc_in, starts[0])
+    for k in range(EARLY, STRIPS):
+        send_piece(k)
+    strips(0, 2, acc_a, 0, first)
+    arrive([copy])
+    arrive(plane_share(acc_in, starts[0]))
+    arrive(core_share(acc_in, starts[0]))
+
+    scale = 1.0 / columns
+    for at, (i, k) in enumerate(inner):
+        tall, wide = slice(i * BLOCK, (i + 1) * BLOCK), slice(k * BLOCK, (k + 1) * BLOCK)
+        work[tall, wide] = total_ref[starts[0] + at * BLOCK : starts[0] + (at + 1) * BLOCK, :] * scale
+    lead_ref[...] = jnp.zeros_like(lead_ref)
+    inverse_ref[...] = jnp.zeros_like(inverse_ref)
+    row = lax.broadcasted_iota(jnp.int32, (BLOCK, BLOCK), 0)
+    column = lax.broadcasted_iota(jnp.int32, (BLOCK, BLOCK), 1)
+    for step in range(per):
+        at, below = step * BLOCK, (step + 1) * BLOCK
+        load_augmented(aug, work[at:below, at:below])
+        eliminate([aug])
+        lead_ref[at:below, at:below] = jnp.where(row <= column, aug[:, 0:BLOCK], 0.0).T
+        inverse = aug[:, BLOCK : 2 * BLOCK]
+        inverse_ref[at:below, at:below] = inverse
+        if step > 0:
+            inverse_ref[at:below, 0:at] = -exact(inverse, exact(lead_ref[at:below, 0:at], inverse_ref[0:at, 0:at], NN), NN)
+        if below < rows:
+            left = exact(work[below:rows, at:below], inverse, NT)
+            lead_ref[below:rows, at:below] = left
+            work[below:rows, below:rows] = work[below:rows, below:rows] - exact(left, left, NT)
+        if step == 0:
+            strips(2, 4, acc_a, 0, first)
+    strips(4, STRIPS - LATE, acc_a, 0, first)
+    fill(acc_a, first * per)
+    core_add(acc_a, slots[2], core_send(acc_a, slots[2]))
+    copies = plane_send(acc_a, slots[3])
+    for k in range(STRIPS - LATE, STRIPS - 1):
+        strips(k, k + 1, acc_b, first, rows - first)
+    plane_add(acc_a, slots[3], copies, starts[1])
+    copy_a = swap(acc_a, starts[1])
+    strips(STRIPS - 1, STRIPS, acc_b, first, rows - first)
+    fill(acc_b, (rows - first) * per)
+    core_add(acc_b, slots[4], core_send(acc_b, slots[4]))
+    copies = plane_send(acc_b, slots[5])
+    arrive([copy_a])
+    copies_a = plane_share(acc_a, starts[1])
+    plane_add(acc_b, slots[5], copies, starts[2])
+    copies = direct_share(acc_b, starts[2])
+    arrive(copies_a)
+    copies_a = core_share(acc_a, starts[1])
+    arrive(copies)
+    copies = core_share(acc_b, starts[2])
+    arrive(copies_a)
+    arrive(copies)
+    for copy in pending:
+        copy.wait_send()
+    for copy in outgoing:
+        copy.wait()
+
+
+def fast_gather(tensor, columns):
+    cols = lax.axis_size("col")
+    rows, _, length = tensor.shape
+    width = length // 2
+    chips = cols // 2
+    _, _, _, _, extents, _, packed = fast_layout(rows, cols)
+    slots = []
+    for extent in extents:
+        slots.append(pltpu.VMEM((extent // 2, BLOCK), jnp.float32))
+        slots.append(pltpu.VMEM((chips - 1, extent // cols, BLOCK), jnp.float32))
+    vmem = pl.BlockSpec(memory_space=pltpu.VMEM)
+    return pl.pallas_call(
+        functools.partial(fast_gather_kernel, cols, columns),
+        out_shape=(
+            jax.ShapeDtypeStruct((rows, width), jnp.float32),
+            jax.ShapeDtypeStruct((packed, BLOCK), jnp.float32),
+            jax.ShapeDtypeStruct((rows, rows), jnp.float32),
+            jax.ShapeDtypeStruct((rows, rows), jnp.float32),
+        ),
+        in_specs=[pl.BlockSpec(memory_space=pl.ANY)],
+        out_specs=(pl.BlockSpec(memory_space=pl.ANY), vmem, vmem, vmem),
+        scratch_shapes=[
+            pltpu.VMEM((rows, length), jnp.float32),
+            pltpu.VMEM((rows, width), jnp.float32),
+            pltpu.VMEM((rows, width), jnp.bfloat16),
+            pltpu.VMEM((rows, width), jnp.bfloat16),
+            pltpu.VMEM((rows, rows), jnp.float32),
+            pltpu.VMEM((rows, rows), jnp.float32),
+            pltpu.VMEM((rows, rows), jnp.float32),
+            pltpu.VMEM((BLOCK, 2 * BLOCK), jnp.float32),
+            *[pltpu.VMEM((extent, BLOCK), jnp.float32) for extent in extents],
+            *slots,
+            pltpu.SemaphoreType.DMA((SEMAPHORES,)),
+        ],
+        compiler_params=pltpu.CompilerParams(collective_id=0, has_side_effects=True),
+        name="fast_gather",
+    )(tensor)
+
+
+def fast_linear_kernel(cols, columns, total_ref, lead_ref, inverse_ref, start_ref, x_ref, recv_ref, factor_ref, basis_ref, core_ref, gram, work, image, aug_f, aug_b, flat, core, flat_sem, core_sem):
+    mode = lax.axis_index("mode")
+    size, rank = start_ref.shape
+    rows = size // 2
+    width = recv_ref.shape[1]
+    per, _, first, inner, extents, starts, _ = fast_layout(rows, cols)
+    own = pl.ds(pl.multiple_of(mode * rows, rows), rows)
+    away = pl.ds(pl.multiple_of((1 - mode) * rows, rows), rows)
+    half = pl.ds(pl.multiple_of(mode * width, width), width)
+    loads = [
+        pltpu.make_async_copy(x_ref.at[:, 0, half], flat.at[own, :], flat_sem.at[0]),
+        pltpu.make_async_copy(recv_ref, flat.at[away, :], flat_sem.at[1]),
+    ]
+    for load in loads:
+        load.start()
+
+    scale = 1.0 / columns
+    for m in range(2):
+        for at, (i, k) in enumerate(inner):
+            begin = starts[0] + m * extents[0] + at * BLOCK
+            block = total_ref[begin : begin + BLOCK, :] * scale
+            tall = slice(m * rows + i * BLOCK, m * rows + (i + 1) * BLOCK)
+            wide = slice(m * rows + k * BLOCK, m * rows + (k + 1) * BLOCK)
+            gram[tall, wide] = block
+            if i != k:
+                gram[wide, tall] = block.T
+    pair = []
+    for m in range(2):
+        blocks = []
+        for c in range(per):
+            a = starts[1] + m * extents[1] + c * first
+            b = starts[2] + m * extents[2] + c * (rows - first)
+            blocks.append(jnp.concatenate([total_ref[a : a + first, :], total_ref[b : b + rows - first, :]], axis=0))
+        pair.append(jnp.concatenate(blocks, axis=1))
+    lower = (pair[0] + pair[1].T) * scale
+    gram[rows:size, 0:rows] = lower
+    gram[0:rows, rows:size] = lower.T
+
+    row = lax.broadcasted_iota(jnp.int32, (BLOCK, BLOCK), 0)
+    column = lax.broadcasted_iota(jnp.int32, (BLOCK, BLOCK), 1)
+    factor_ref[0:rows, 0:rows] = lead_ref[...]
+    factor_ref[0:rows, rows:size] = jnp.zeros((rows, rows), jnp.float32)
+    left = exact(lower, inverse_ref[...], NT)
+    factor_ref[rows:size, 0:rows] = left
+    work[...] = gram[rows:size, rows:size] - exact(left, left, NT)
+
+    for step in range(max(per, POWER)):
+        augs = []
+        at, below = step * BLOCK, (step + 1) * BLOCK
+        if step < POWER:
+            source = start_ref if step == 0 else basis_ref
+            image[...] = exact(gram[...], source[...], NN)
+            load_augmented(aug_b, exact(image[...], image[...], TN))
+            augs.append(aug_b)
+        if step < per:
+            load_augmented(aug_f, work[at:below, at:below])
+            augs.append(aug_f)
+        eliminate(augs)
+        if step < POWER:
+            basis_ref[...] = exact(image[...], aug_b[:, rank : 2 * rank], NT)
+        if step < per:
+            upper = jnp.where(row <= column, aug_f[:, 0:BLOCK], 0.0)
+            factor_ref[rows + at : rows + below, rows + at : rows + below] = upper.T
+            if step > 0:
+                factor_ref[rows : rows + at, rows + at : rows + below] = jnp.zeros((at, BLOCK), jnp.float32)
+            if below < rows:
+                left = exact(work[below:rows, at:below], aug_f[:, BLOCK : 2 * BLOCK], NT)
+                factor_ref[rows + below : size, rows + at : rows + below] = left
+                work[below:rows, below:rows] = work[below:rows, below:rows] - exact(left, left, NT)
+
+    for load in loads:
+        load.wait()
+    high, low = halves(basis_ref[...])
+    piece = min(CHUNK, width)
+    copies = []
+    for start in range(0, width, piece):
+        part = slice(start, start + piece)
+        flat_high, flat_low = halves(flat[:, part])
+        core[:, part] = contract(high, flat_high, TN) + contract(high, flat_low, TN) + contract(low, flat_high, TN)
+        copy = pltpu.make_async_copy(core.at[:, part], core_ref.at[:, 0, part], core_sem.at[len(copies)])
+        copy.start()
+        copies.append(copy)
+    for copy in copies:
+        copy.wait()
+
+
+def fast_linear(columns, total, lead, inverse, start_basis, tensor, recv):
+    size, rank = start_basis.shape
+    rows, width = recv.shape
+    vmem = pl.BlockSpec(memory_space=pltpu.VMEM)
+    anywhere = pl.BlockSpec(memory_space=pl.ANY)
+    return pl.pallas_call(
+        functools.partial(fast_linear_kernel, lax.axis_size("col"), columns),
+        out_shape=(
+            jax.ShapeDtypeStruct((size, size), jnp.float32),
+            jax.ShapeDtypeStruct((size, rank), jnp.float32),
+            jax.ShapeDtypeStruct((rank, 1, width), jnp.float32),
+        ),
+        in_specs=[vmem, vmem, vmem, vmem, anywhere, anywhere],
+        out_specs=(vmem, vmem, anywhere),
+        scratch_shapes=[
+            pltpu.VMEM((size, size), jnp.float32),
+            pltpu.VMEM((rows, rows), jnp.float32),
+            pltpu.VMEM((size, rank), jnp.float32),
+            pltpu.VMEM((BLOCK, 2 * BLOCK), jnp.float32),
+            pltpu.VMEM((rank, 2 * rank), jnp.float32),
+            pltpu.VMEM((size, width), jnp.float32),
+            pltpu.VMEM((rank, width), jnp.float32),
+            pltpu.SemaphoreType.DMA((2,)),
+            pltpu.SemaphoreType.DMA((width // min(CHUNK, width),)),
+        ],
+        name="fast_linear",
+    )(total, lead, inverse, start_basis, tensor, recv)
+
+
 def per_device(tensor, start_basis):
+    modes, cols = lax.axis_size("mode"), lax.axis_size("col")
     depth = tensor.shape[1]
+    columns = depth * tensor.shape[2] * cols
+    if fast_case(modes, cols, tensor.shape):
+        recv, total, lead, inverse = fast_gather(tensor, columns)
+        return fast_linear(columns, total, lead, inverse, start_basis, tensor, recv)
     flat, packed = gather(tensor)
-    columns = flat.shape[1] * lax.axis_size("mode") * lax.axis_size("col")
-    factor, basis, core = linear(columns, depth, packed, start_basis, flat)
-    return (factor, basis, core)
+    return linear(columns, depth, packed, start_basis, flat)
 
 
 def solution(mesh):

time: 113 us -> 94.3 us (0.83)
  Pallas kernels: 112 us -> 93.4 us
    pallas_call x2, Pallas kernels: 112 us -> 93.4 us  [the longest x1 69.2 us: fast_gather(): pl.pallas_call(functools.partial(fast_gather_kernel, cols, columns), out_...]
where the time goes in v1:
time: 94.3 us; the launch traced here: 94.2 us
  Pallas kernels  93.4 us (99%)
    pallas_call x1, Pallas kernels, fast_gather(): pl.pallas_call(functools.partial(fast_gather_kernel, cols, columns), out_...  69.2 us
    pallas_call x1, Pallas kernels, fast_linear(): pl.pallas_call(functools.partial(fast_linear_kernel, lax.axis_size('col')...  24.2 us

profile of v1, /device:TPU:0, one launch (start us, length us, event | category | flops | bytes accessed | tf_op | source)
XLA Modules:
  0.0 94.2 jit_solution(10697043036721241092)
XLA Ops:
  0.6 69.2 %fast_gather.1 = (f32[256,2048]{1,0:T(8,128)}, f32[1792,128]{1,0:T(8,128)}, f32[256,256]{1,0:T(8,128)}, f32[256,256]{1,0:T(8,128)}) custom-call(f32[256,1,4096]{2,1,0:T(1,128)} %x_ref.3), custom_call_target="tpu_custom_call" | custom-call | tf_op jit(solution)/shard_map/fast_gather/pallas_call | solution.py:737
  69.8 24.2 %fast_linear.1 = (f32[512,512]{1,0:T(8,128)}, f32[512,128]{1,0:T(8,128)}, f32[128,1,2048]{2,1,0:T(1,128)}) custom-call(f32[1792,128]{1,0:T(8,128)} %get-tuple-element.7.total_ref, f32[256,256]{1,0:T(8,128)} %get-tuple-element.8.lead_ref, f32[256,256]{1,0:T(8,128)} %get-tuple-element.9.inverse_ref, f32[512,128]{1,0:T(8,128)} %start_ref.1, ...), custom_call_target="tpu_custom_call" | custom-call | tf_op jit(solution)/shard_map/fast_linear/pallas_call | solution.py:856

commit v2 on v1

--- a/solution.py
+++ b/solution.py
@@ -43,37 +43,51 @@
     return high, middle, rest - middle
 
 
+def spread(tile, lane):
+    return jnp.broadcast_to(tile[:, lane : lane + 1], tile.shape)
+
+
 def eliminate_panel(aug, j):
-    size, width = aug.shape
+    parts, size, _ = aug.shape
     first = PANEL * j
-    rows = [aug[first + t : first + t + 1, :] for t in range(PANEL)]
+    after = first + PANEL
+    below = after + PANEL
+    rows = [[aug[p, pl.ds(first + t, PANEL, stride=0), :] for p in range(parts)] for t in range(PANEL)]
     entry = {}
+    for s in range(PANEL):
+        for t in range(s + 1):
+            entry[s, t] = spread(rows[t][0], first + s)
+    if after < size:
+        following = [aug[p, after:below, :] for p in range(parts)]
+        column = [spread(following[0], first + t) for t in range(PANEL)]
     for t in range(PANEL):
-        for s in range(t, PANEL):
-            value = rows[t][:, first + s : first + s + 1]
-            entry[s, t] = jnp.broadcast_to(value, (1, size))
-    pivots = []
-    for t in range(PANEL):
-        pivot = entry[t, t]
-        pivots.append(pivot)
-        inverse = 1.0 / pivot
+        inverse = 1.0 / entry[t, t]
         for s in range(t + 1, PANEL):
             ratio = entry[s, t] * inverse
             for u in range(s, PANEL):
                 entry[u, s] = entry[u, s] - ratio * entry[u, t]
-            rows[s] = rows[s] - jnp.concatenate([ratio] * (width // size), axis=1) * rows[t]
-    done = []
-    for t in range(PANEL):
-        scale = lax.rsqrt(pivots[t])
-        done.append(rows[t] * jnp.concatenate([scale] * (width // size), axis=1))
-    panel = jnp.concatenate(done, axis=0)
-    aug[first : first + PANEL, :] = panel
-    below = first + PANEL
+            rows[s] = [a - ratio * b for a, b in zip(rows[s], rows[t])]
+        scale = lax.rsqrt(entry[t, t])
+        for p in range(parts):
+            aug[p, first + t : first + t + 1, :] = (rows[t][p] * scale)[0:1]
+        if after < size:
+            ratio = column[t] * inverse
+            for u in range(t + 1, PANEL):
+                column[u] = column[u] - ratio * entry[u, t]
+            following = [a - ratio * b for a, b in zip(following, rows[t])]
+    if after < size:
+        for p in range(parts):
+            aug[p, after:below, :] = following[p]
     if below < size:
-        high, middle, low = split3(panel)
-        left = jnp.concatenate([high, high, middle, high, low, middle], axis=0).astype(jnp.bfloat16)
-        right = jnp.concatenate([high, middle, high, low, high, middle], axis=0).astype(jnp.bfloat16)
-        aug[below:size, :] = aug[below:size, :] - contract(left[:, below:size], right, TN)
+        rights = []
+        for p in range(parts):
+            high, middle, low = split3(aug[p, first:after, :])
+            if p == 0:
+                left = jnp.concatenate([high, high, middle, high, low, middle], axis=0).astype(jnp.bfloat16)
+            rights.append(jnp.concatenate([high, middle, high, low, high, middle], axis=0).astype(jnp.bfloat16))
+        update = contract(left, jnp.concatenate(rights, axis=1), TN)
+        for p in range(parts):
+            aug[p, below:size, :] = aug[p, below:size, :] - update[below:size, p * size : (p + 1) * size]
 
 
 def eliminate(augs):
@@ -84,10 +98,11 @@
 
 def load_augmented(aug, matrix):
     size = matrix.shape[0]
-    row = lax.broadcasted_iota(jnp.int32, (size, size), 0)
-    column = lax.broadcasted_iota(jnp.int32, (size, size), 1)
-    aug[:, 0:size] = matrix
-    aug[:, size : 2 * size] = jnp.where(row == column, 1.0, 0.0).astype(jnp.float32)
+    aug[0] = matrix
+    if aug.shape[0] > 1:
+        row = lax.broadcasted_iota(jnp.int32, (size, size), 0)
+        column = lax.broadcasted_iota(jnp.int32, (size, size), 1)
+        aug[1] = jnp.where(row == column, 1.0, 0.0).astype(jnp.float32)
 
 
 def lower_blocks(blocks):
@@ -418,15 +433,15 @@
             augs.append(aug_b)
         eliminate(augs)
         if step < POWER:
-            basis_ref[...] = exact(image[...], aug_b[:, rank : 2 * rank], NT)
+            basis_ref[...] = exact(image[...], aug_b[1], NT)
         if step < blocks:
-            upper = jnp.where(row <= column, aug_f[:, 0:BLOCK], 0.0)
+            upper = jnp.where(row <= column, aug_f[0], 0.0)
             factor_ref[at : at + BLOCK, at : at + BLOCK] = upper.T
             if step > 0:
                 factor_ref[0:at, at : at + BLOCK] = jnp.zeros((at, BLOCK), jnp.float32)
             below = at + BLOCK
             if below < size:
-                inverse = aug_f[:, BLOCK : 2 * BLOCK]
+                inverse = aug_f[1]
                 left = exact(work[below:size, at : at + BLOCK], inverse, NT)
                 factor_ref[below:size, at : at + BLOCK] = left
                 work[below:size, below:size] = work[below:size, below:size] - exact(left, left, NT)
@@ -467,8 +482,8 @@
             pltpu.VMEM((size, size), jnp.float32),
             pltpu.VMEM((size, size), jnp.float32),
             pltpu.VMEM((size, rank), jnp.float32),
-            pltpu.VMEM((BLOCK, 2 * BLOCK), jnp.float32),
-            pltpu.VMEM((rank, 2 * rank), jnp.float32),
+            pltpu.VMEM((2, BLOCK, BLOCK), jnp.float32),
+            pltpu.VMEM((2, rank, rank), jnp.float32),
             pltpu.VMEM((rank, flat.shape[1]), jnp.float32),
             pltpu.SemaphoreType.DMA((flat.shape[1] // min(CHUNK, length),)),
         ],
@@ -478,13 +493,18 @@
 
 def fast_case(modes, cols, shape):
     rows, depth, length = shape
-    return modes == 2 and depth == 1 and rows % (2 * BLOCK) == 0 and cols % 2 == 0 and cols > 2 and length % (2 * BLOCK) == 0
+    return modes == 2 and depth == 1 and rows % (2 * BLOCK) == 0 and cols % 4 == 0 and length % (2 * BLOCK) == 0
 
 
 STRIPS = 8
-LATE = 2
+LATE = 4
 EARLY = 3
-SEMAPHORES = 240
+HELD = 2
+PIECES = STRIPS + 2
+
+
+def fast_cuts(strip):
+    return sorted([k * strip for k in range(STRIPS + 1)] + [2 * strip + strip // 2, 6 * strip + strip // 2])
 
 
 def fast_layout(rows, cols):
@@ -501,8 +521,8 @@
     return per, strip, first, inner, extents, starts, at
 
 
-def fast_gather_kernel(cols, columns, x_ref, recv_out, total_ref, lead_ref, inverse_ref, local, recv, own_high, own_low, main, cross, work, aug, acc_in, acc_a, acc_b, *rest):
-    slots, sems = rest[:-1], rest[-1]
+def fast_gather_kernel(cols, columns, x_ref, recv_out, early_out, lead_out, inverse_out, late_ref, local, recv, early_ref, lead_ref, inverse_ref, own_high, own_low, main, cross, work, aug, acc_in, acc_a, acc_b, *rest):
+    slots, sems, hello = rest[:-2], rest[-2], rest[-1]
     mode, col = lax.axis_index("mode"), lax.axis_index("col")
     other_mode = 1 - mode
     rows, _, length = x_ref.shape
@@ -510,19 +530,25 @@
     chips = cols // 2
     per, strip, first, inner, extents, starts, _ = fast_layout(rows, cols)
     core, chip = lax.rem(col, 2), lax.div(col, 2)
-    counter = [0]
-    pending = []
-
-    def sem():
-        counter[0] += 1
-        return sems.at[counter[0] - 1]
-
-    def push(source, target, device):
+    names = {}
+    pending = {}
+
+    def sem(*name):
+        return sems.at[names.setdefault(name, len(names))]
+
+    def drain(*kinds):
+        for name in [name for name in pending if name[0] in kinds]:
+            pending.pop(name).wait_send()
+
+    def push(source, target, device, *name):
+        if name in pending:
+            pending.pop(name).wait_send()
         copy = pltpu.make_async_remote_copy(
-            src_ref=source, dst_ref=target, send_sem=sem(), recv_sem=sem(), device_id=device, device_id_type=MESH
+            src_ref=source, dst_ref=target, send_sem=sem("send", *name), recv_sem=sem("recv", *name),
+            device_id=device, device_id_type=MESH,
         )
         copy.start()
-        pending.append(copy)
+        pending[name] = copy
         return copy
 
     sibling = (mode, chip * 2 + 1 - core)
@@ -531,20 +557,42 @@
     for d in range(1, chips):
         place = lax.rem(chip + d, chips)
         plane.append((place, (mode, place * 2 + core)))
-    across = [(other_mode, lax.rem(chip + d, chips) * 2 + core) for d in range(chips)]
-
-    greeted = [sibling] + [device for _, device in plane] + across
+
+    line = chips // 2
+    place = lax.div(chip, 2)
+    beside = (mode, (place * 2 + 1 - lax.rem(chip, 2)) * 2 + core)
+    above, under = (mode, col + 4), (mode, col - 4)
+    has_above, has_under = place < line - 1, place > 0
+
+    def hail(semaphore, device):
+        pl.semaphore_signal(semaphore, inc=1, device_id=device, device_id_type=MESH)
+
     barrier = pltpu.get_barrier_semaphore()
-    for device in greeted:
-        pl.semaphore_signal(barrier, inc=1, device_id=device, device_id_type=MESH)
-    pl.semaphore_wait(barrier, len(greeted))
+    for device in (partner, sibling, beside):
+        hail(barrier, device)
+    pl.when(has_above)(lambda: hail(barrier, above))
+    pl.when(has_under)(lambda: hail(barrier, under))
+    pl.semaphore_wait(barrier, 3 + has_above.astype(jnp.int32) + has_under.astype(jnp.int32))
+
+    def meet_line():
+        pl.when(has_under)(lambda: pl.semaphore_wait(hello.at[0], 1))
+        pl.when(has_above)(lambda: hail(hello.at[0], above))
+        pl.when(has_above)(lambda: pl.semaphore_wait(hello.at[1], 1))
+        pl.when(has_under)(lambda: hail(hello.at[1], under))
+        hail(hello.at[2], beside)
+
+    def meet_beside():
+        pl.semaphore_wait(hello.at[2], 1)
 
     pieces = []
     away = pl.ds(pl.multiple_of(other_mode * width, width), width)
 
+    cuts = fast_cuts(strip)
+
     def send_piece(k):
-        span = slice(k * strip, (k + 1) * strip)
-        pieces.append(push(x_ref.at[span, 0, away], recv.at[span, :], partner))
+        span = slice(cuts[k], cuts[k + 1])
+        pieces.append(push(x_ref.at[span, 0, away], recv.at[span, :], partner, "piece", k))
+        del pending["piece", k]
 
     for k in range(EARLY):
         send_piece(k)
@@ -553,10 +601,12 @@
     part = length // 4
     for c in range(4):
         span = slice(c * part, (c + 1) * part)
-        copy = pltpu.make_async_copy(x_ref.at[:, 0, span], local.at[:, span], sem())
+        copy = pltpu.make_async_copy(x_ref.at[:, 0, span], local.at[:, span], sem("local", c))
         copy.start()
         loads.append(copy)
     for c in range(4):
+        if c == 1:
+            meet_line()
         loads[c].wait()
         high, low = halves(local[:, c * part : (c + 1) * part])
         if c == 0:
@@ -579,7 +629,7 @@
 
     def core_send(acc, slot):
         half = acc.shape[0] // 2
-        return push(acc.at[rows_at((1 - core) * half, half), :], slot.at[...], sibling)
+        return push(acc.at[rows_at((1 - core) * half, half), :], slot.at[...], sibling, "core")
 
     def core_add(acc, slot, copy):
         half = acc.shape[0] // 2
@@ -592,10 +642,10 @@
         share = half // chips
         copies = []
         for d, (place, device) in enumerate(plane):
-            copies.append(push(acc.at[rows_at(core * half + place * share, share), :], slot.at[d], device))
+            copies.append(push(acc.at[rows_at(core * half + place * share, share), :], slot.at[d], device, "plane", d))
         return copies
 
-    def plane_add(acc, slot, copies, start):
+    def plane_add(acc, slot, copies, total, start):
         half = acc.shape[0] // 2
         share = half // chips
         base = core * half + chip * share
@@ -604,58 +654,64 @@
         added = acc[rows_at(base, share), :]
         for d in range(chips - 1):
             added = added + slot[d]
-        total_ref[rows_at(start + mode * acc.shape[0] + base, share), :] = added
-
-    def swap(acc, start):
+        total[rows_at(start + mode * acc.shape[0] + base, share), :] = added
+
+    def swap(acc, total, start, phase):
         half = acc.shape[0] // 2
         share = half // chips
         mine = rows_at(start + mode * acc.shape[0] + core * half + chip * share, share)
-        return push(total_ref.at[mine, :], total_ref.at[mine, :], partner)
-
-    def plane_share(acc, start):
+        return push(total.at[mine, :], total.at[mine, :], partner, "swap", phase)
+
+    def plane_share(acc, total, start, modes):
         half = acc.shape[0] // 2
         share = half // chips
         copies = []
-        for _, device in plane:
-            for m in range(2):
+        for d, (_, device) in enumerate(plane):
+            for at, m in modes:
                 mine = rows_at(start + m * acc.shape[0] + core * half + chip * share, share)
-                copies.append(push(total_ref.at[mine, :], total_ref.at[mine, :], device))
+                copies.append(push(total.at[mine, :], total.at[mine, :], device, "share", d, at))
         return copies
 
-    def direct_share(acc, start):
-        half = acc.shape[0] // 2
-        share = half // chips
-        mine = rows_at(start + mode * acc.shape[0] + core * half + chip * share, share)
-        devices = [device for _, device in plane] + across
-        return [push(total_ref.at[mine, :], total_ref.at[mine, :], device) for device in devices]
-
-    def core_share(acc, start):
+    def core_share(acc, total, start):
         half = acc.shape[0] // 2
         copies = []
         for m in range(2):
             mine = rows_at(start + m * acc.shape[0] + core * half, half)
-            copies.append(push(total_ref.at[mine, :], total_ref.at[mine, :], sibling))
+            copies.append(push(total.at[mine, :], total.at[mine, :], sibling, "both", m))
         return copies
 
     def arrive(copies):
         for copy in copies:
             copy.wait_recv()
 
-    outgoing = []
+    outgoing = {}
+    leaving = [0]
+    both = [(0, 0), (1, 1)]
+
+    def leave(source, target):
+        lane = leaving[0] % len(loads)
+        leaving[0] += 1
+        if lane in outgoing:
+            outgoing.pop(lane).wait()
+        copy = pltpu.make_async_copy(source, target, sem("local", lane))
+        copy.start()
+        outgoing[lane] = copy
 
     def strips(begin, end, acc, offset, tall):
-        arrive(pieces[begin:end])
         span = slice(begin * strip, end * strip)
-        copy = pltpu.make_async_copy(recv.at[span, :], recv_out.at[span, :], sem())
-        copy.start()
-        outgoing.append(copy)
+        arrive(pieces[cuts.index(begin * strip) : cuts.index(end * strip)])
+        leave(recv.at[span, :], recv_out.at[span, :])
         high, low = halves(recv[span, :])
-        value = contract(high, own_high[...], NT) + (contract(high, own_low[...], NT) + contract(low, own_high[...], NT))
+        both = contract(own_high[...], jnp.concatenate([high, low], axis=0), NT)
+        count = high.shape[0]
+        value = both[:, 0:count] + (both[:, count:] + contract(own_low[...], high, NT))
+        value = value.T
         for c in range(per):
             at = c * tall + begin * strip - offset
             acc[at : at + (end - begin) * strip, :] = value[:, c * BLOCK : (c + 1) * BLOCK]
 
     fill(acc_in, len(inner) * BLOCK)
+    meet_beside()
     copy = core_send(acc_in, slots[0])
     mine = local[:, pl.ds(pl.multiple_of(mode * width, width), width)]
     high, low = halves(mine)
@@ -663,19 +719,22 @@
     own_low[...] = low
     core_add(acc_in, slots[0], copy)
     copies = plane_send(acc_in, slots[1])
-    plane_add(acc_in, slots[1], copies, starts[0])
-    copy = swap(acc_in, starts[0])
-    for k in range(EARLY, STRIPS):
+    plane_add(acc_in, slots[1], copies, early_ref, starts[0])
+    copy = swap(acc_in, early_ref, starts[0], 0)
+    for k in range(EARLY, PIECES - HELD):
         send_piece(k)
-    strips(0, 2, acc_a, 0, first)
+    strips(0, 1, acc_a, 0, first)
     arrive([copy])
-    arrive(plane_share(acc_in, starts[0]))
-    arrive(core_share(acc_in, starts[0]))
+    copies = plane_share(acc_in, early_ref, starts[0], both)
+    drain("core", "plane", "swap")
+    strips(1, 2, acc_a, 0, first)
+    arrive(copies)
+    arrive(core_share(acc_in, early_ref, starts[0]))
 
     scale = 1.0 / columns
     for at, (i, k) in enumerate(inner):
         tall, wide = slice(i * BLOCK, (i + 1) * BLOCK), slice(k * BLOCK, (k + 1) * BLOCK)
-        work[tall, wide] = total_ref[starts[0] + at * BLOCK : starts[0] + (at + 1) * BLOCK, :] * scale
+        work[tall, wide] = early_ref[starts[0] + at * BLOCK : starts[0] + (at + 1) * BLOCK, :] * scale
     lead_ref[...] = jnp.zeros_like(lead_ref)
     inverse_ref[...] = jnp.zeros_like(inverse_ref)
     row = lax.broadcasted_iota(jnp.int32, (BLOCK, BLOCK), 0)
@@ -684,8 +743,8 @@
         at, below = step * BLOCK, (step + 1) * BLOCK
         load_augmented(aug, work[at:below, at:below])
         eliminate([aug])
-        lead_ref[at:below, at:below] = jnp.where(row <= column, aug[:, 0:BLOCK], 0.0).T
-        inverse = aug[:, BLOCK : 2 * BLOCK]
+        lead_ref[at:below, at:below] = jnp.where(row <= column, aug[0], 0.0).T
+        inverse = aug[1]
         inverse_ref[at:below, at:below] = inverse
         if step > 0:
             inverse_ref[at:below, 0:at] = -exact(inverse, exact(lead_ref[at:below, 0:at], inverse_ref[0:at, 0:at], NN), NN)
@@ -694,33 +753,47 @@
             lead_ref[below:rows, at:below] = left
             work[below:rows, below:rows] = work[below:rows, below:rows] - exact(left, left, NT)
         if step == 0:
-            strips(2, 4, acc_a, 0, first)
-    strips(4, STRIPS - LATE, acc_a, 0, first)
-    fill(acc_a, first * per)
-    core_add(acc_a, slots[2], core_send(acc_a, slots[2]))
-    copies = plane_send(acc_a, slots[3])
-    for k in range(STRIPS - LATE, STRIPS - 1):
-        strips(k, k + 1, acc_b, first, rows - first)
-    plane_add(acc_a, slots[3], copies, starts[1])
-    copy_a = swap(acc_a, starts[1])
+            strips(2, STRIPS - LATE, acc_a, 0, first)
+            fill(acc_a, first * per)
+            core_add(acc_a, slots[2], core_send(acc_a, slots[2]))
+            copies = plane_send(acc_a, slots[3])
+    plane_add(acc_a, slots[3], copies, early_ref, starts[1])
+    copy = swap(acc_a, early_ref, starts[1], 1)
+    for k in range(PIECES - HELD, PIECES):
+        send_piece(k)
+    leave(lead_ref, lead_out)
+    leave(inverse_ref, inverse_out)
+    strips(STRIPS - LATE, STRIPS - 2, acc_b, first, rows - first)
+    arrive([copy])
+    copies = plane_share(acc_a, early_ref, starts[1], both)
+    drain("core", "plane", "swap", "both")
+    for copy in pieces[:-HELD]:
+        copy.wait_send()
+    strips(STRIPS - 2, STRIPS - 1, acc_b, first, rows - first)
+    arrive(copies)
+    copies = core_share(acc_a, early_ref, starts[1])
+    drain("share")
+    arrive(copies)
+    leave(early_ref, early_out)
     strips(STRIPS - 1, STRIPS, acc_b, first, rows - first)
     fill(acc_b, (rows - first) * per)
     core_add(acc_b, slots[4], core_send(acc_b, slots[4]))
-    copies = plane_send(acc_b, slots[5])
-    arrive([copy_a])
-    copies_a = plane_share(acc_a, starts[1])
-    plane_add(acc_b, slots[5], copies, starts[2])
-    copies = direct_share(acc_b, starts[2])
-    arrive(copies_a)
-    copies_a = core_share(acc_a, starts[1])
+    plane_add(acc_b, slots[5], plane_send(acc_b, slots[5]), late_ref, 0)
+    copy = swap(acc_b, late_ref, 0, 2)
+    copies = plane_share(acc_b, late_ref, 0, [(0, mode)])
+    drain("core", "plane", "both")
+    arrive([copy])
+    copies += plane_share(acc_b, late_ref, 0, [(1, other_mode)])
+    drain("swap")
+    for copy in pieces[-HELD:]:
+        copy.wait_send()
+    for copy in outgoing.values():
+        copy.wait()
     arrive(copies)
-    copies = core_share(acc_b, starts[2])
-    arrive(copies_a)
+    copies = core_share(acc_b, late_ref, 0)
+    drain("share")
     arrive(copies)
-    for copy in pending:
-        copy.wait_send()
-    for copy in outgoing:
-        copy.wait()
+    drain("both")
 
 
 def fast_gather(tensor, columns):
@@ -728,41 +801,47 @@
     rows, _, length = tensor.shape
     width = length // 2
     chips = cols // 2
-    _, _, _, _, extents, _, packed = fast_layout(rows, cols)
+    _, _, _, _, extents, starts, _ = fast_layout(rows, cols)
     slots = []
     for extent in extents:
         slots.append(pltpu.VMEM((extent // 2, BLOCK), jnp.float32))
         slots.append(pltpu.VMEM((chips - 1, extent // cols, BLOCK), jnp.float32))
     vmem = pl.BlockSpec(memory_space=pltpu.VMEM)
+    anywhere = pl.BlockSpec(memory_space=pl.ANY)
     return pl.pallas_call(
         functools.partial(fast_gather_kernel, cols, columns),
         out_shape=(
             jax.ShapeDtypeStruct((rows, width), jnp.float32),
-            jax.ShapeDtypeStruct((packed, BLOCK), jnp.float32),
+            jax.ShapeDtypeStruct((starts[2], BLOCK), jnp.float32),
             jax.ShapeDtypeStruct((rows, rows), jnp.float32),
             jax.ShapeDtypeStruct((rows, rows), jnp.float32),
+            jax.ShapeDtypeStruct((2 * extents[2], BLOCK), jnp.float32),
         ),
-        in_specs=[pl.BlockSpec(memory_space=pl.ANY)],
-        out_specs=(pl.BlockSpec(memory_space=pl.ANY), vmem, vmem, vmem),
+        in_specs=[anywhere],
+        out_specs=(anywhere, anywhere, anywhere, anywhere, vmem),
         scratch_shapes=[
             pltpu.VMEM((rows, length), jnp.float32),
             pltpu.VMEM((rows, width), jnp.float32),
+            pltpu.VMEM((starts[2], BLOCK), jnp.float32),
+            pltpu.VMEM((rows, rows), jnp.float32),
+            pltpu.VMEM((rows, rows), jnp.float32),
             pltpu.VMEM((rows, width), jnp.bfloat16),
             pltpu.VMEM((rows, width), jnp.bfloat16),
             pltpu.VMEM((rows, rows), jnp.float32),
             pltpu.VMEM((rows, rows), jnp.float32),
             pltpu.VMEM((rows, rows), jnp.float32),
-            pltpu.VMEM((BLOCK, 2 * BLOCK), jnp.float32),
+            pltpu.VMEM((2, BLOCK, BLOCK), jnp.float32),
             *[pltpu.VMEM((extent, BLOCK), jnp.float32) for extent in extents],
             *slots,
-            pltpu.SemaphoreType.DMA((SEMAPHORES,)),
+            pltpu.SemaphoreType.DMA((2 * PIECES + 16 + 6 * (chips - 1),)),
+            pltpu.SemaphoreType.REGULAR((3,)),
         ],
         compiler_params=pltpu.CompilerParams(collective_id=0, has_side_effects=True),
         name="fast_gather",
     )(tensor)
 
 
-def fast_linear_kernel(cols, columns, total_ref, lead_ref, inverse_ref, start_ref, x_ref, recv_ref, factor_ref, basis_ref, core_ref, gram, work, image, aug_f, aug_b, flat, core, flat_sem, core_sem):
+def fast_linear_kernel(cols, columns, early_ref, late_ref, lead_ref, inverse_ref, start_ref, x_ref, recv_ref, factor_ref, basis_ref, core_ref, gram, work, image, aug_f, aug_last, aug_b, flat, core, flat_sem, core_sem):
     mode = lax.axis_index("mode")
     size, rank = start_ref.shape
     rows = size // 2
@@ -774,6 +853,7 @@
     loads = [
         pltpu.make_async_copy(x_ref.at[:, 0, half], flat.at[own, :], flat_sem.at[0]),
         pltpu.make_async_copy(recv_ref, flat.at[away, :], flat_sem.at[1]),
+        pltpu.make_async_copy(lead_ref, factor_ref.at[0:rows, 0:rows], flat_sem.at[2]),
     ]
     for load in loads:
         load.start()
@@ -782,7 +862,7 @@
     for m in range(2):
         for at, (i, k) in enumerate(inner):
             begin = starts[0] + m * extents[0] + at * BLOCK
-            block = total_ref[begin : begin + BLOCK, :] * scale
+            block = early_ref[begin : begin + BLOCK, :] * scale
             tall = slice(m * rows + i * BLOCK, m * rows + (i + 1) * BLOCK)
             wide = slice(m * rows + k * BLOCK, m * rows + (k + 1) * BLOCK)
             gram[tall, wide] = block
@@ -793,8 +873,8 @@
         blocks = []
         for c in range(per):
             a = starts[1] + m * extents[1] + c * first
-            b = starts[2] + m * extents[2] + c * (rows - first)
-            blocks.append(jnp.concatenate([total_ref[a : a + first, :], total_ref[b : b + rows - first, :]], axis=0))
+            b = m * extents[2] + c * (rows - first)
+            blocks.append(jnp.concatenate([early_ref[a : a + first, :], late_ref[b : b + rows - first, :]], axis=0))
         pair.append(jnp.concatenate(blocks, axis=1))
     lower = (pair[0] + pair[1].T) * scale
     gram[rows:size, 0:rows] = lower
@@ -802,7 +882,6 @@
 
     row = lax.broadcasted_iota(jnp.int32, (BLOCK, BLOCK), 0)
     column = lax.broadcasted_iota(jnp.int32, (BLOCK, BLOCK), 1)
-    factor_ref[0:rows, 0:rows] = lead_ref[...]
     factor_ref[0:rows, rows:size] = jnp.zeros((rows, rows), jnp.float32)
     left = exact(lower, inverse_ref[...], NT)
     factor_ref[rows:size, 0:rows] = left
@@ -817,18 +896,19 @@
             load_augmented(aug_b, exact(image[...], image[...], TN))
             augs.append(aug_b)
         if step < per:
-            load_augmented(aug_f, work[at:below, at:below])
-            augs.append(aug_f)
+            block = aug_f if below < rows else aug_last
+            load_augmented(block, work[at:below, at:below])
+            augs.append(block)
         eliminate(augs)
         if step < POWER:
-            basis_ref[...] = exact(image[...], aug_b[:, rank : 2 * rank], NT)
+            basis_ref[...] = exact(image[...], aug_b[1], NT)
         if step < per:
-            upper = jnp.where(row <= column, aug_f[:, 0:BLOCK], 0.0)
+            upper = jnp.where(row <= column, block[0], 0.0)
             factor_ref[rows + at : rows + below, rows + at : rows + below] = upper.T
             if step > 0:
                 factor_ref[rows : rows + at, rows + at : rows + below] = jnp.zeros((at, BLOCK), jnp.float32)
             if below < rows:
-                left = exact(work[below:rows, at:below], aug_f[:, BLOCK : 2 * BLOCK], NT)
+                left = exact(work[below:rows, at:below], aug_f[1], NT)
                 factor_ref[rows + below : size, rows + at : rows + below] = left
                 work[below:rows, below:rows] = work[below:rows, below:rows] - exact(left, left, NT)
 
@@ -848,7 +928,7 @@
         copy.wait()
 
 
-def fast_linear(columns, total, lead, inverse, start_basis, tensor, recv):
+def fast_linear(columns, early, late, lead, inverse, start_basis, tensor, recv):
     size, rank = start_basis.shape
     rows, width = recv.shape
     vmem = pl.BlockSpec(memory_space=pltpu.VMEM)
@@ -860,21 +940,22 @@
             jax.ShapeDtypeStruct((size, rank), jnp.float32),
             jax.ShapeDtypeStruct((rank, 1, width), jnp.float32),
         ),
-        in_specs=[vmem, vmem, vmem, vmem, anywhere, anywhere],
+        in_specs=[vmem, vmem, anywhere, vmem, vmem, anywhere, anywhere],
         out_specs=(vmem, vmem, anywhere),
         scratch_shapes=[
             pltpu.VMEM((size, size), jnp.float32),
             pltpu.VMEM((rows, rows), jnp.float32),
             pltpu.VMEM((size, rank), jnp.float32),
-            pltpu.VMEM((BLOCK, 2 * BLOCK), jnp.float32),
-            pltpu.VMEM((rank, 2 * rank), jnp.float32),
+            pltpu.VMEM((2, BLOCK, BLOCK), jnp.float32),
+            pltpu.VMEM((1, BLOCK, BLOCK), jnp.float32),
+            pltpu.VMEM((2, rank, rank), jnp.float32),
             pltpu.VMEM((size, width), jnp.float32),
             pltpu.VMEM((rank, width), jnp.float32),
-            pltpu.SemaphoreType.DMA((2,)),
+            pltpu.SemaphoreType.DMA((3,)),
             pltpu.SemaphoreType.DMA((width // min(CHUNK, width),)),
         ],
         name="fast_linear",
-    )(total, lead, inverse, start_basis, tensor, recv)
+    )(early, late, lead, inverse, start_basis, tensor, recv)
 
 
 def per_device(tensor, start_basis):
@@ -882,8 +963,8 @@
     depth = tensor.shape[1]
     columns = depth * tensor.shape[2] * cols
     if fast_case(modes, cols, tensor.shape):
-        recv, total, lead, inverse = fast_gather(tensor, columns)
-        return fast_linear(columns, total, lead, inverse, start_basis, tensor, recv)
+        recv, early, lead, inverse, late = fast_gather(tensor, columns)
+        return fast_linear(columns, early, late, lead, inverse, start_basis, tensor, recv)
     flat, packed = gather(tensor)
     return linear(columns, depth, packed, start_basis, flat)
 

time: 94.3 us -> 87 us (0.923)
  Pallas kernels: 93.4 us -> 86 us
    pallas_call x1, Pallas kernels: 24.2 us -> 20.1 us  [fast_linear(): pl.pallas_call(functools.partial(fast_linear_kernel, lax.axis_size('col')...]
    pallas_call x1, Pallas kernels: 69.2 us -> 65.9 us  [fast_gather(): pl.pallas_call(functools.partial(fast_gather_kernel, cols, columns), out_...]
where the time goes in v2:
time: 87 us; the launch traced here: 86.8 us
  Pallas kernels  86 us (99%)
    pallas_call x1, Pallas kernels, fast_gather(): pl.pallas_call(functools.partial(fast_gather_kernel, cols, columns), out_...  65.9 us
    pallas_call x1, Pallas kernels, fast_linear(): pl.pallas_call(functools.partial(fast_linear_kernel, lax.axis_size('col')...  20.1 us

profile of v2, /device:TPU:0, one launch (start us, length us, event | category | flops | bytes accessed | tf_op | source)
XLA Modules:
  0.0 86.8 jit_solution(12541730426603638584)
XLA Ops:
  0.6 65.9 %fast_gather.1 = (f32[256,2048]{1,0:T(8,128)}, f32[1280,128]{1,0:T(8,128)}, f32[256,256]{1,0:T(8,128)}, f32[256,256]{1,0:T(8,128)}, f32[512,128]{1,0:T(8,128)}) custom-call(f32[256,1,4096]{2,1,0:T(1,128)} %x_ref.3), custom_call_target="tpu_custom_call" | custom-call | tf_op jit(solution)/shard_map/fast_gather/pallas_call | solution.py:811
  66.6 20.1 %fast_linear.1 = (f32[512,512]{1,0:T(8,128)}, f32[512,128]{1,0:T(8,128)}, f32[128,1,2048]{2,1,0:T(1,128)}) custom-call(f32[1280,128]{1,0:T(8,128)} %get-tuple-element.8.early_ref, f32[512,128]{1,0:T(8,128)} %get-tuple-element.9.late_ref, f32[256,256]{1,0:T(8,128)} %get-tuple-element.10.lead_ref, f32[256,256]{1,0:T(8,128)} %get-tuple-element.11.inverse_ref, ...), custom_call_target="tpu_custom_call" | custom-call | tf_op jit(solution)/shard_map/fast_linear/pallas_call | solution.py:936

commit v3 on v2

--- a/solution.py
+++ b/solution.py
@@ -34,6 +34,38 @@
 NN = ((1,), (0,))
 NT = ((1,), (1,))
 TN = ((0,), (0,))
+
+
+def thirds(value):
+    high = value.astype(jnp.bfloat16)
+    rest = value - high.astype(jnp.float32)
+    middle = rest.astype(jnp.bfloat16)
+    low = (rest - middle.astype(jnp.float32)).astype(jnp.bfloat16)
+    return high, middle, low
+
+
+def six_terms(left, right, dims):
+    high, middle, low = right
+    beside, along = (1, 0) if dims == NN else (0, 1)
+    wide = jnp.concatenate([high, middle], axis=beside)
+    first = contract(
+        jnp.concatenate([left[0], left[1]], axis=1), jnp.concatenate([wide, wide], axis=along), dims
+    )
+    second = contract(
+        jnp.concatenate([left[2], left[0]], axis=1), jnp.concatenate([high, low], axis=along), dims
+    )
+    count = second.shape[1]
+    return first[:, 0:count] + (first[:, count:] + second)
+
+
+def self_product(parts):
+    high, middle, low = parts
+    pair = jnp.concatenate([high, middle], axis=1)
+    product = contract(pair, pair, TN)
+    small = contract(high, low, TN)
+    count = small.shape[0]
+    rest = (product[0:count, count:] + product[count:, 0:count]) + (product[count:, count:] + (small + small.T))
+    return product[0:count, 0:count] + rest
 
 
 def split3(value):
@@ -521,7 +553,7 @@
     return per, strip, first, inner, extents, starts, at
 
 
-def fast_gather_kernel(cols, columns, x_ref, recv_out, early_out, lead_out, inverse_out, late_ref, local, recv, early_ref, lead_ref, inverse_ref, own_high, own_low, main, cross, work, aug, acc_in, acc_a, acc_b, *rest):
+def fast_gather_kernel(cols, columns, x_ref, high_out, low_out, early_out, lead_out, inverse_out, late_ref, local, recv, early_ref, lead_ref, inverse_ref, own_high, own_low, other_high, other_low, main, cross, work, aug, acc_in, acc_a, acc_b, *rest):
     slots, sems, hello = rest[:-2], rest[-2], rest[-1]
     mode, col = lax.axis_index("mode"), lax.axis_index("col")
     other_mode = 1 - mode
@@ -700,8 +732,12 @@
     def strips(begin, end, acc, offset, tall):
         span = slice(begin * strip, end * strip)
         arrive(pieces[cuts.index(begin * strip) : cuts.index(end * strip)])
-        leave(recv.at[span, :], recv_out.at[span, :])
         high, low = halves(recv[span, :])
+        other_high[span, :] = high
+        other_low[span, :] = low
+        target = pl.ds(pl.multiple_of(other_mode * rows + begin * strip, strip), (end - begin) * strip)
+        leave(other_high.at[span, :], high_out.at[target, :])
+        leave(other_low.at[span, :], low_out.at[target, :])
         both = contract(own_high[...], jnp.concatenate([high, low], axis=0), NT)
         count = high.shape[0]
         value = both[:, 0:count] + (both[:, count:] + contract(own_low[...], high, NT))
@@ -719,6 +755,9 @@
     own_low[...] = low
     core_add(acc_in, slots[0], copy)
     copies = plane_send(acc_in, slots[1])
+    target = pl.ds(pl.multiple_of(mode * rows, rows), rows)
+    leave(own_high, high_out.at[target, :])
+    leave(own_low, low_out.at[target, :])
     plane_add(acc_in, slots[1], copies, early_ref, starts[0])
     copy = swap(acc_in, early_ref, starts[0], 0)
     for k in range(EARLY, PIECES - HELD):
@@ -811,22 +850,22 @@
     return pl.pallas_call(
         functools.partial(fast_gather_kernel, cols, columns),
         out_shape=(
-            jax.ShapeDtypeStruct((rows, width), jnp.float32),
+            jax.ShapeDtypeStruct((2 * rows, width), jnp.bfloat16),
+            jax.ShapeDtypeStruct((2 * rows, width), jnp.bfloat16),
             jax.ShapeDtypeStruct((starts[2], BLOCK), jnp.float32),
             jax.ShapeDtypeStruct((rows, rows), jnp.float32),
             jax.ShapeDtypeStruct((rows, rows), jnp.float32),
             jax.ShapeDtypeStruct((2 * extents[2], BLOCK), jnp.float32),
         ),
         in_specs=[anywhere],
-        out_specs=(anywhere, anywhere, anywhere, anywhere, vmem),
+        out_specs=(anywhere, anywhere, anywhere, anywhere, anywhere, vmem),
         scratch_shapes=[
             pltpu.VMEM((rows, length), jnp.float32),
             pltpu.VMEM((rows, width), jnp.float32),
             pltpu.VMEM((starts[2], BLOCK), jnp.float32),
             pltpu.VMEM((rows, rows), jnp.float32),
             pltpu.VMEM((rows, rows), jnp.float32),
-            pltpu.VMEM((rows, width), jnp.bfloat16),
-            pltpu.VMEM((rows, width), jnp.bfloat16),
+            *[pltpu.VMEM((rows, width), jnp.bfloat16)] * 4,
             pltpu.VMEM((rows, rows), jnp.float32),
             pltpu.VMEM((rows, rows), jnp.float32),
             pltpu.VMEM((rows, rows), jnp.float32),
@@ -841,19 +880,15 @@
     )(tensor)
 
 
-def fast_linear_kernel(cols, columns, early_ref, late_ref, lead_ref, inverse_ref, start_ref, x_ref, recv_ref, factor_ref, basis_ref, core_ref, gram, work, image, aug_f, aug_last, aug_b, flat, core, flat_sem, core_sem):
-    mode = lax.axis_index("mode")
+def fast_linear_kernel(cols, columns, early_ref, late_ref, lead_ref, inverse_ref, start_ref, high_ref, low_ref, factor_ref, basis_ref, core_ref, gram, split, work, aug_f, aug_last, aug_b, flat_high, flat_low, core, flat_sem, core_sem):
     size, rank = start_ref.shape
     rows = size // 2
-    width = recv_ref.shape[1]
+    width = core_ref.shape[2]
     per, _, first, inner, extents, starts, _ = fast_layout(rows, cols)
-    own = pl.ds(pl.multiple_of(mode * rows, rows), rows)
-    away = pl.ds(pl.multiple_of((1 - mode) * rows, rows), rows)
-    half = pl.ds(pl.multiple_of(mode * width, width), width)
     loads = [
-        pltpu.make_async_copy(x_ref.at[:, 0, half], flat.at[own, :], flat_sem.at[0]),
-        pltpu.make_async_copy(recv_ref, flat.at[away, :], flat_sem.at[1]),
-        pltpu.make_async_copy(lead_ref, factor_ref.at[0:rows, 0:rows], flat_sem.at[2]),
+        pltpu.make_async_copy(lead_ref, factor_ref.at[0:rows, 0:rows], flat_sem.at[0]),
+        pltpu.make_async_copy(high_ref, flat_high, flat_sem.at[1]),
+        pltpu.make_async_copy(low_ref, flat_low, flat_sem.at[2]),
     ]
     for load in loads:
         load.start()
@@ -879,21 +914,24 @@
     lower = (pair[0] + pair[1].T) * scale
     gram[rows:size, 0:rows] = lower
     gram[0:rows, rows:size] = lower.T
+    for p, part in enumerate(thirds(gram[...])):
+        split[p] = part
 
     row = lax.broadcasted_iota(jnp.int32, (BLOCK, BLOCK), 0)
     column = lax.broadcasted_iota(jnp.int32, (BLOCK, BLOCK), 1)
     factor_ref[0:rows, rows:size] = jnp.zeros((rows, rows), jnp.float32)
-    left = exact(lower, inverse_ref[...], NT)
+    left = six_terms([split[p, rows:size, 0:rows] for p in range(3)], thirds(inverse_ref[...]), NT)
     factor_ref[rows:size, 0:rows] = left
-    work[...] = gram[rows:size, rows:size] - exact(left, left, NT)
-
+    parts = thirds(left)
+    work[...] = gram[rows:size, rows:size] - six_terms(parts, parts, NT)
+
+    basis = start_ref[...]
     for step in range(max(per, POWER)):
         augs = []
         at, below = step * BLOCK, (step + 1) * BLOCK
         if step < POWER:
-            source = start_ref if step == 0 else basis_ref
-            image[...] = exact(gram[...], source[...], NN)
-            load_augmented(aug_b, exact(image[...], image[...], TN))
+            image = thirds(six_terms([split[p] for p in range(3)], thirds(basis), NN))
+            load_augmented(aug_b, self_product(image))
             augs.append(aug_b)
         if step < per:
             block = aug_f if below < rows else aug_last
@@ -901,26 +939,29 @@
             augs.append(block)
         eliminate(augs)
         if step < POWER:
-            basis_ref[...] = exact(image[...], aug_b[1], NT)
+            basis = six_terms(image, thirds(aug_b[1]), NT)
         if step < per:
             upper = jnp.where(row <= column, block[0], 0.0)
             factor_ref[rows + at : rows + below, rows + at : rows + below] = upper.T
             if step > 0:
                 factor_ref[rows : rows + at, rows + at : rows + below] = jnp.zeros((at, BLOCK), jnp.float32)
             if below < rows:
-                left = exact(work[below:rows, at:below], aug_f[1], NT)
+                left = six_terms(thirds(work[below:rows, at:below]), thirds(aug_f[1]), NT)
                 factor_ref[rows + below : size, rows + at : rows + below] = left
-                work[below:rows, below:rows] = work[below:rows, below:rows] - exact(left, left, NT)
-
+                parts = thirds(left)
+                work[below:rows, below:rows] = work[below:rows, below:rows] - six_terms(parts, parts, NT)
+
+    basis_ref[...] = basis
     for load in loads:
         load.wait()
-    high, low = halves(basis_ref[...])
+    high, low = halves(basis)
+    both = jnp.concatenate([high, low], axis=1)
     piece = min(CHUNK, width)
     copies = []
     for start in range(0, width, piece):
         part = slice(start, start + piece)
-        flat_high, flat_low = halves(flat[:, part])
-        core[:, part] = contract(high, flat_high, TN) + contract(high, flat_low, TN) + contract(low, flat_high, TN)
+        product = contract(both, flat_high[:, part], TN)
+        core[:, part] = product[0:rank] + (product[rank:] + contract(high, flat_low[:, part], TN))
         copy = pltpu.make_async_copy(core.at[:, part], core_ref.at[:, 0, part], core_sem.at[len(copies)])
         copy.start()
         copies.append(copy)
@@ -928,9 +969,9 @@
         copy.wait()
 
 
-def fast_linear(columns, early, late, lead, inverse, start_basis, tensor, recv):
+def fast_linear(columns, early, late, lead, inverse, start_basis, high, low):
     size, rank = start_basis.shape
-    rows, width = recv.shape
+    rows, width = size // 2, high.shape[1]
     vmem = pl.BlockSpec(memory_space=pltpu.VMEM)
     anywhere = pl.BlockSpec(memory_space=pl.ANY)
     return pl.pallas_call(
@@ -944,18 +985,19 @@
         out_specs=(vmem, vmem, anywhere),
         scratch_shapes=[
             pltpu.VMEM((size, size), jnp.float32),
+            pltpu.VMEM((3, size, size), jnp.bfloat16),
             pltpu.VMEM((rows, rows), jnp.float32),
-            pltpu.VMEM((size, rank), jnp.float32),
             pltpu.VMEM((2, BLOCK, BLOCK), jnp.float32),
             pltpu.VMEM((1, BLOCK, BLOCK), jnp.float32),
             pltpu.VMEM((2, rank, rank), jnp.float32),
-            pltpu.VMEM((size, width), jnp.float32),
+            pltpu.VMEM((size, width), jnp.bfloat16),
+            pltpu.VMEM((size, width), jnp.bfloat16),
             pltpu.VMEM((rank, width), jnp.float32),
             pltpu.SemaphoreType.DMA((3,)),
             pltpu.SemaphoreType.DMA((width // min(CHUNK, width),)),
         ],
         name="fast_linear",
-    )(early, late, lead, inverse, start_basis, tensor, recv)
+    )(early, late, lead, inverse, start_basis, high, low)
 
 
 def per_device(tensor, start_basis):
@@ -963,8 +1005,8 @@
     depth = tensor.shape[1]
     columns = depth * tensor.shape[2] * cols
     if fast_case(modes, cols, tensor.shape):
-        recv, early, lead, inverse, late = fast_gather(tensor, columns)
-        return fast_linear(columns, early, late, lead, inverse, start_basis, tensor, recv)
+        high, low, early, lead, inverse, late = fast_gather(tensor, columns)
+        return fast_linear(columns, early, late, lead, inverse, start_basis, high, low)
     flat, packed = gather(tensor)
     return linear(columns, depth, packed, start_basis, flat)
 

time: 87 us -> 84.5 us (0.971)
  Pallas kernels: 86 us -> 83.5 us
    pallas_call x1, Pallas kernels: 20.1 us -> 17.5 us  [fast_linear(): pl.pallas_call(functools.partial(fast_linear_kernel, lax.axis_size('col')...]
where the time goes in v3:
time: 84.5 us; the launch traced here: 84.3 us
  Pallas kernels  83.5 us (99%)
    pallas_call x1, Pallas kernels, fast_gather(): pl.pallas_call(functools.partial(fast_gather_kernel, cols, columns), out_...  66 us
    pallas_call x1, Pallas kernels, fast_linear(): pl.pallas_call(functools.partial(fast_linear_kernel, lax.axis_size('col')...  17.5 us

profile of v3, /device:TPU:0, one launch (start us, length us, event | category | flops | bytes accessed | tf_op | source)
XLA Modules:
  0.0 84.3 jit_solution(1713090656808707026)
XLA Ops:
  0.6 66.0 %fast_gather.1 = (bf16[512,2048]{1,0:T(8,128)(2,1)}, bf16[512,2048]{1,0:T(8,128)(2,1)}, f32[1280,128]{1,0:T(8,128)}, f32[256,256]{1,0:T(8,128)}, f32[256,256]{1,0:T(8,128)}, /*index=5*/f32[512,128]{1,0:T(8,128)}) custom-call(f32[256,1,4096]{2,1,0:T(1,128)} %x_ref.1), custom_call_target="tpu_custom_call" | custom-call | tf_op jit(solution)/shard_map/fast_gather/pallas_call | solution.py:850
  66.6 17.5 %fast_linear.1 = (f32[512,512]{1,0:T(8,128)}, f32[512,128]{1,0:T(8,128)}, f32[128,1,2048]{2,1,0:T(1,128)}) custom-call(f32[1280,128]{1,0:T(8,128)} %get-tuple-element.9.early_ref, f32[512,128]{1,0:T(8,128)} %get-tuple-element.10.late_ref, f32[256,256]{1,0:T(8,128)} %get-tuple-element.11.lead_ref, f32[256,256]{1,0:T(8,128)} %get-tuple-element.12.inverse_ref, ...), custom_call_target="tpu_custom_call" | custom-call | tf_op jit(solution)/shard_map/fast_linear/pallas_call | solution.py:977

commit v4 on v3

--- a/solution.py
+++ b/solution.py
@@ -1,4 +1,5 @@
 import functools
+import itertools
 
 import jax
 import jax.numpy as jnp
@@ -615,6 +616,10 @@
 
     def meet_beside():
         pl.semaphore_wait(hello.at[2], 1)
+        hail(hello.at[3], partner)
+
+    def meet_across():
+        pl.semaphore_wait(hello.at[3], 1)
 
     pieces = []
     away = pl.ds(pl.multiple_of(other_mode * width, width), width)
@@ -704,6 +709,16 @@
                 copies.append(push(total.at[mine, :], total.at[mine, :], device, "share", d, at))
         return copies
 
+    def direct_share(acc, total, start):
+        half = acc.shape[0] // 2
+        share = half // chips
+        mine = rows_at(start + mode * acc.shape[0] + core * half + chip * share, share)
+        copies = []
+        for d in range(chips):
+            device = (other_mode, lax.rem(chip + d, chips) * 2 + core)
+            copies.append(push(total.at[mine, :], total.at[mine, :], device, "across", d))
+        return copies
+
     def core_share(acc, total, start):
         half = acc.shape[0] // 2
         copies = []
@@ -759,6 +774,7 @@
     leave(own_high, high_out.at[target, :])
     leave(own_low, low_out.at[target, :])
     plane_add(acc_in, slots[1], copies, early_ref, starts[0])
+    meet_across()
     copy = swap(acc_in, early_ref, starts[0], 0)
     for k in range(EARLY, PIECES - HELD):
         send_piece(k)
@@ -818,19 +834,15 @@
     fill(acc_b, (rows - first) * per)
     core_add(acc_b, slots[4], core_send(acc_b, slots[4]))
     plane_add(acc_b, slots[5], plane_send(acc_b, slots[5]), late_ref, 0)
-    copy = swap(acc_b, late_ref, 0, 2)
-    copies = plane_share(acc_b, late_ref, 0, [(0, mode)])
+    copies = direct_share(acc_b, late_ref, 0) + plane_share(acc_b, late_ref, 0, [(0, mode)])
     drain("core", "plane", "both")
-    arrive([copy])
-    copies += plane_share(acc_b, late_ref, 0, [(1, other_mode)])
-    drain("swap")
     for copy in pieces[-HELD:]:
         copy.wait_send()
     for copy in outgoing.values():
         copy.wait()
     arrive(copies)
     copies = core_share(acc_b, late_ref, 0)
-    drain("share")
+    drain("share", "across")
     arrive(copies)
     drain("both")
 
@@ -872,15 +884,15 @@
             pltpu.VMEM((2, BLOCK, BLOCK), jnp.float32),
             *[pltpu.VMEM((extent, BLOCK), jnp.float32) for extent in extents],
             *slots,
-            pltpu.SemaphoreType.DMA((2 * PIECES + 16 + 6 * (chips - 1),)),
-            pltpu.SemaphoreType.REGULAR((3,)),
+            pltpu.SemaphoreType.DMA((2 * PIECES + 16 + 8 * (chips - 1),)),
+            pltpu.SemaphoreType.REGULAR((4,)),
         ],
         compiler_params=pltpu.CompilerParams(collective_id=0, has_side_effects=True),
         name="fast_gather",
     )(tensor)
 
 
-def fast_linear_kernel(cols, columns, early_ref, late_ref, lead_ref, inverse_ref, start_ref, high_ref, low_ref, factor_ref, basis_ref, core_ref, gram, split, work, aug_f, aug_last, aug_b, flat_high, flat_low, core, flat_sem, core_sem):
+def fast_linear_kernel(cols, columns, early_ref, late_ref, lead_ref, inverse_ref, start_ref, high_ref, low_ref, factor_out, basis_out, core_ref, factor_ref, basis_ref, gram, split, work, aug_f, aug_last, aug_b, flat_high, flat_low, core, flat_sem, out_sem, core_sem):
     size, rank = start_ref.shape
     rows = size // 2
     width = core_ref.shape[2]
@@ -920,27 +932,53 @@
     row = lax.broadcasted_iota(jnp.int32, (BLOCK, BLOCK), 0)
     column = lax.broadcasted_iota(jnp.int32, (BLOCK, BLOCK), 1)
     factor_ref[0:rows, rows:size] = jnp.zeros((rows, rows), jnp.float32)
-    left = six_terms([split[p, rows:size, 0:rows] for p in range(3)], thirds(inverse_ref[...]), NT)
-    factor_ref[rows:size, 0:rows] = left
-    parts = thirds(left)
-    work[...] = gram[rows:size, rows:size] - six_terms(parts, parts, NT)
-
-    basis = start_ref[...]
-    for step in range(max(per, POWER)):
-        augs = []
-        at, below = step * BLOCK, (step + 1) * BLOCK
-        if step < POWER:
+    outgoing = []
+
+    def leave(source, target, semaphore):
+        copy = pltpu.make_async_copy(source, target, semaphore)
+        copy.start()
+        outgoing.append(copy)
+
+    def basis_chain():
+        basis = start_ref[...]
+        for _ in range(POWER):
             image = thirds(six_terms([split[p] for p in range(3)], thirds(basis), NN))
             load_augmented(aug_b, self_product(image))
-            augs.append(aug_b)
-        if step < per:
+            yield
+            for j in range(rank // PANEL):
+                eliminate_panel(aug_b, j)
+                yield
+            basis = six_terms(image, thirds(aug_b[1]), NT)
+            yield
+        basis_ref[...] = basis
+        leave(basis_ref, basis_out, out_sem.at[3])
+        for load in loads[1:]:
+            load.wait()
+        high, low = halves(basis)
+        both = jnp.concatenate([high, low], axis=1)
+        piece = min(CHUNK, width)
+        for n, start in enumerate(range(0, width, piece)):
+            part = slice(start, start + piece)
+            product = contract(both, flat_high[:, part], TN)
+            core[:, part] = product[0:rank] + (product[rank:] + contract(high, flat_low[:, part], TN))
+            leave(core.at[:, part], core_ref.at[:, 0, part], core_sem.at[n])
+            yield
+
+    def factor_chain():
+        left = six_terms([split[p, rows:size, 0:rows] for p in range(3)], thirds(inverse_ref[...]), NT)
+        factor_ref[rows:size, 0:rows] = left
+        leave(factor_ref.at[rows:size, 0:rows], factor_out.at[rows:size, 0:rows], out_sem.at[0])
+        yield
+        parts = thirds(left)
+        work[...] = gram[rows:size, rows:size] - six_terms(parts, parts, NT)
+        yield
+        for step in range(per):
+            at, below = step * BLOCK, (step + 1) * BLOCK
             block = aug_f if below < rows else aug_last
             load_augmented(block, work[at:below, at:below])
-            augs.append(block)
-        eliminate(augs)
-        if step < POWER:
-            basis = six_terms(image, thirds(aug_b[1]), NT)
-        if step < per:
+            for j in range(BLOCK // PANEL):
+                eliminate_panel(block, j)
+                yield
             upper = jnp.where(row <= column, block[0], 0.0)
             factor_ref[rows + at : rows + below, rows + at : rows + below] = upper.T
             if step > 0:
@@ -950,22 +988,14 @@
                 factor_ref[rows + below : size, rows + at : rows + below] = left
                 parts = thirds(left)
                 work[below:rows, below:rows] = work[below:rows, below:rows] - six_terms(parts, parts, NT)
-
-    basis_ref[...] = basis
-    for load in loads:
-        load.wait()
-    high, low = halves(basis)
-    both = jnp.concatenate([high, low], axis=1)
-    piece = min(CHUNK, width)
-    copies = []
-    for start in range(0, width, piece):
-        part = slice(start, start + piece)
-        product = contract(both, flat_high[:, part], TN)
-        core[:, part] = product[0:rank] + (product[rank:] + contract(high, flat_low[:, part], TN))
-        copy = pltpu.make_async_copy(core.at[:, part], core_ref.at[:, 0, part], core_sem.at[len(copies)])
-        copy.start()
-        copies.append(copy)
-    for copy in copies:
+            yield
+        loads[0].wait()
+        leave(factor_ref.at[0:rows, :], factor_out.at[0:rows, :], out_sem.at[1])
+        leave(factor_ref.at[rows:size, rows:size], factor_out.at[rows:size, rows:size], out_sem.at[2])
+
+    for _ in itertools.zip_longest(basis_chain(), factor_chain()):
+        pass
+    for copy in outgoing:
         copy.wait()
 
 
@@ -982,8 +1012,10 @@
             jax.ShapeDtypeStruct((rank, 1, width), jnp.float32),
         ),
         in_specs=[vmem, vmem, anywhere, vmem, vmem, anywhere, anywhere],
-        out_specs=(vmem, vmem, anywhere),
+        out_specs=(anywhere, anywhere, anywhere),
         scratch_shapes=[
+            pltpu.VMEM((size, size), jnp.float32),
+            pltpu.VMEM((size, rank), jnp.float32),
             pltpu.VMEM((size, size), jnp.float32),
             pltpu.VMEM((3, size, size), jnp.bfloat16),
             pltpu.VMEM((rows, rows), jnp.float32),
@@ -994,6 +1026,7 @@
             pltpu.VMEM((size, width), jnp.bfloat16),
             pltpu.VMEM((rank, width), jnp.float32),
             pltpu.SemaphoreType.DMA((3,)),
+            pltpu.SemaphoreType.DMA((4,)),
             pltpu.SemaphoreType.DMA((width // min(CHUNK, width),)),
         ],
         name="fast_linear",

time: 84.5 us -> 81.9 us (0.969)
  Pallas kernels: 83.5 us -> 80.9 us
    pallas_call x1, Pallas kernels: 17.5 us -> 15.6 us  [fast_linear(): pl.pallas_call(functools.partial(fast_linear_kernel, lax.axis_size('col')...]
where the time goes in v4:
time: 81.9 us; the launch traced here: 81.7 us
  Pallas kernels  80.9 us (99%)
    pallas_call x1, Pallas kernels, fast_gather(): pl.pallas_call(functools.partial(fast_gather_kernel, cols, columns), out_...  65.3 us
    pallas_call x1, Pallas kernels, fast_linear(): pl.pallas_call(functools.partial(fast_linear_kernel, lax.axis_size('col')...  15.6 us

profile of v4, /device:TPU:0, one launch (start us, length us, event | category | flops | bytes accessed | tf_op | source)
XLA Modules:
  0.0 81.7 jit_solution(5419797378841304766)
XLA Ops:
  0.6 65.3 %fast_gather.1 = (bf16[512,2048]{1,0:T(8,128)(2,1)}, bf16[512,2048]{1,0:T(8,128)(2,1)}, f32[1280,128]{1,0:T(8,128)}, f32[256,256]{1,0:T(8,128)}, f32[256,256]{1,0:T(8,128)}, /*index=5*/f32[512,128]{1,0:T(8,128)}) custom-call(f32[256,1,4096]{2,1,0:T(1,128)} %x_ref.1), custom_call_target="tpu_custom_call" | custom-call | tf_op jit(solution)/shard_map/fast_gather/pallas_call | solution.py:862
  65.9 15.6 %fast_linear.1 = (f32[512,512]{1,0:T(8,128)}, f32[512,128]{1,0:T(8,128)}, f32[128,1,2048]{2,1,0:T(1,128)}) custom-call(f32[1280,128]{1,0:T(8,128)} %get-tuple-element.9.early_ref, f32[512,128]{1,0:T(8,128)} %get-tuple-element.10.late_ref, f32[256,256]{1,0:T(8,128)} %get-tuple-element.11.lead_ref, f32[256,256]{1,0:T(8,128)} %get-tuple-element.12.inverse_ref, ...), custom_call_target="tpu_custom_call" | custom-call | tf_op jit(solution)/shard_map/fast_linear/pallas_call | solution.py:1007

commit v5 on v4

--- a/solution.py
+++ b/solution.py
@@ -532,8 +532,8 @@
 STRIPS = 8
 LATE = 4
 EARLY = 3
-HELD = 2
-PIECES = STRIPS + 2
+HELD = 3
+PIECES = STRIPS + 3
 
 
 def fast_cuts(strip):
@@ -584,6 +584,21 @@
         pending[name] = copy
         return copy
 
+    def volley(name, triples, whole):
+        if (name,) in pending:
+            pending.pop((name,)).wait_send()
+
+        def copy_of(source, target, device):
+            return pltpu.make_async_remote_copy(
+                src_ref=source, dst_ref=target, send_sem=sem("send", name), recv_sem=sem("recv", name),
+                device_id=device, device_id_type=MESH,
+            )
+
+        for triple in triples:
+            copy_of(*triple).start()
+        pending[(name,)] = copy_of(whole, whole, sibling)
+        return [pending[(name,)]]
+
     sibling = (mode, chip * 2 + 1 - core)
     partner = (other_mode, col)
     plane = []
@@ -626,10 +641,20 @@
 
     cuts = fast_cuts(strip)
 
+    def piece_of(source, target, k):
+        return pltpu.make_async_remote_copy(
+            src_ref=source, dst_ref=target, send_sem=sem("pieces"), recv_sem=sem("piece", k),
+            device_id=partner, device_id_type=MESH,
+        )
+
     def send_piece(k):
-        span = slice(cuts[k], cuts[k + 1])
-        pieces.append(push(x_ref.at[span, 0, away], recv.at[span, :], partner, "piece", k))
-        del pending["piece", k]
+        if k < PIECES - 2:
+            span, start, count = slice(cuts[k], cuts[k + 1]), 0, width
+        else:
+            span, start, count = slice(rows - strip, rows), (k - PIECES + 2) * (width // 2), width // 2
+        source = pl.ds(pl.multiple_of(other_mode * width + start, BLOCK), count)
+        pieces.append(piece_of(x_ref.at[span, 0, source], recv.at[span, start : start + count], k))
+        pieces[k].start()
 
     for k in range(EARLY):
         send_piece(k)
@@ -677,10 +702,10 @@
     def plane_send(acc, slot):
         half = acc.shape[0] // 2
         share = half // chips
-        copies = []
+        triples = []
         for d, (place, device) in enumerate(plane):
-            copies.append(push(acc.at[rows_at(core * half + place * share, share), :], slot.at[d], device, "plane", d))
-        return copies
+            triples.append((acc.at[rows_at(core * half + place * share, share), :], slot.at[d], device))
+        return volley("plane", triples, slot)
 
     def plane_add(acc, slot, copies, total, start):
         half = acc.shape[0] // 2
@@ -699,33 +724,32 @@
         mine = rows_at(start + mode * acc.shape[0] + core * half + chip * share, share)
         return push(total.at[mine, :], total.at[mine, :], partner, "swap", phase)
 
-    def plane_share(acc, total, start, modes):
+    def plane_share(acc, total, start):
         half = acc.shape[0] // 2
         share = half // chips
-        copies = []
-        for d, (_, device) in enumerate(plane):
-            for at, m in modes:
+        triples = []
+        for _, device in plane:
+            for m in range(2):
                 mine = rows_at(start + m * acc.shape[0] + core * half + chip * share, share)
-                copies.append(push(total.at[mine, :], total.at[mine, :], device, "share", d, at))
-        return copies
+                triples.append((total.at[mine, :], total.at[mine, :], device))
+        return volley("share", triples, total.at[0 : len(triples) * share, :])
 
     def direct_share(acc, total, start):
         half = acc.shape[0] // 2
         share = half // chips
         mine = rows_at(start + mode * acc.shape[0] + core * half + chip * share, share)
-        copies = []
-        for d in range(chips):
-            device = (other_mode, lax.rem(chip + d, chips) * 2 + core)
-            copies.append(push(total.at[mine, :], total.at[mine, :], device, "across", d))
-        return copies
+        devices = [(other_mode, lax.rem(chip + d, chips) * 2 + core) for d in range(chips)]
+        devices += [device for _, device in plane]
+        triples = [(total.at[mine, :], total.at[mine, :], device) for device in devices]
+        return volley("direct", triples, total.at[0 : len(triples) * share, :])
 
     def core_share(acc, total, start):
         half = acc.shape[0] // 2
-        copies = []
+        triples = []
         for m in range(2):
             mine = rows_at(start + m * acc.shape[0] + core * half, half)
-            copies.append(push(total.at[mine, :], total.at[mine, :], sibling, "both", m))
-        return copies
+            triples.append((total.at[mine, :], total.at[mine, :], sibling))
+        return volley("both", triples, total.at[0 : 2 * half, :])
 
     def arrive(copies):
         for copy in copies:
@@ -733,7 +757,6 @@
 
     outgoing = {}
     leaving = [0]
-    both = [(0, 0), (1, 1)]
 
     def leave(source, target):
         lane = leaving[0] % len(loads)
@@ -746,20 +769,28 @@
 
     def strips(begin, end, acc, offset, tall):
         span = slice(begin * strip, end * strip)
-        arrive(pieces[cuts.index(begin * strip) : cuts.index(end * strip)])
-        high, low = halves(recv[span, :])
-        other_high[span, :] = high
-        other_low[span, :] = low
-        target = pl.ds(pl.multiple_of(other_mode * rows + begin * strip, strip), (end - begin) * strip)
+        if end < STRIPS:
+            steps = [(pieces[cuts.index(begin * strip) : cuts.index(end * strip)], 0, width)]
+        else:
+            steps = [([pieces[-2]], 0, width // 2), ([pieces[-1]], width // 2, width // 2)]
+        count = (end - begin) * strip
+        value = None
+        for copies, start, wide in steps:
+            arrive(copies)
+            part = slice(start, start + wide)
+            high, low = halves(recv[span, part])
+            other_high[span, part] = high
+            other_low[span, part] = low
+            both = contract(own_high[:, part], jnp.concatenate([high, low], axis=0), NT)
+            added = both[:, 0:count] + (both[:, count:] + contract(own_low[:, part], high, NT))
+            value = added if value is None else value + added
+        target = pl.ds(pl.multiple_of(other_mode * rows + begin * strip, strip), count)
         leave(other_high.at[span, :], high_out.at[target, :])
         leave(other_low.at[span, :], low_out.at[target, :])
-        both = contract(own_high[...], jnp.concatenate([high, low], axis=0), NT)
-        count = high.shape[0]
-        value = both[:, 0:count] + (both[:, count:] + contract(own_low[...], high, NT))
         value = value.T
         for c in range(per):
             at = c * tall + begin * strip - offset
-            acc[at : at + (end - begin) * strip, :] = value[:, c * BLOCK : (c + 1) * BLOCK]
+            acc[at : at + count, :] = value[:, c * BLOCK : (c + 1) * BLOCK]
 
     fill(acc_in, len(inner) * BLOCK)
     meet_beside()
@@ -780,7 +811,7 @@
         send_piece(k)
     strips(0, 1, acc_a, 0, first)
     arrive([copy])
-    copies = plane_share(acc_in, early_ref, starts[0], both)
+    copies = plane_share(acc_in, early_ref, starts[0])
     drain("core", "plane", "swap")
     strips(1, 2, acc_a, 0, first)
     arrive(copies)
@@ -820,10 +851,8 @@
     leave(inverse_ref, inverse_out)
     strips(STRIPS - LATE, STRIPS - 2, acc_b, first, rows - first)
     arrive([copy])
-    copies = plane_share(acc_a, early_ref, starts[1], both)
+    copies = plane_share(acc_a, early_ref, starts[1])
     drain("core", "plane", "swap", "both")
-    for copy in pieces[:-HELD]:
-        copy.wait_send()
     strips(STRIPS - 2, STRIPS - 1, acc_b, first, rows - first)
     arrive(copies)
     copies = core_share(acc_a, early_ref, starts[1])
@@ -834,15 +863,14 @@
     fill(acc_b, (rows - first) * per)
     core_add(acc_b, slots[4], core_send(acc_b, slots[4]))
     plane_add(acc_b, slots[5], plane_send(acc_b, slots[5]), late_ref, 0)
-    copies = direct_share(acc_b, late_ref, 0) + plane_share(acc_b, late_ref, 0, [(0, mode)])
+    copies = direct_share(acc_b, late_ref, 0)
     drain("core", "plane", "both")
-    for copy in pieces[-HELD:]:
-        copy.wait_send()
+    piece_of(x_ref.at[:, 0, away], recv, 0).wait_send()
     for copy in outgoing.values():
         copy.wait()
     arrive(copies)
     copies = core_share(acc_b, late_ref, 0)
-    drain("share", "across")
+    drain("direct")
     arrive(copies)
     drain("both")
 
@@ -884,7 +912,7 @@
             pltpu.VMEM((2, BLOCK, BLOCK), jnp.float32),
             *[pltpu.VMEM((extent, BLOCK), jnp.float32) for extent in extents],
             *slots,
-            pltpu.SemaphoreType.DMA((2 * PIECES + 16 + 8 * (chips - 1),)),
+            pltpu.SemaphoreType.DMA((PIECES + 19,)),
             pltpu.SemaphoreType.REGULAR((4,)),
         ],
         compiler_params=pltpu.CompilerParams(collective_id=0, has_side_effects=True),
@@ -892,7 +920,7 @@
     )(tensor)
 
 
-def fast_linear_kernel(cols, columns, early_ref, late_ref, lead_ref, inverse_ref, start_ref, high_ref, low_ref, factor_out, basis_out, core_ref, factor_ref, basis_ref, gram, split, work, aug_f, aug_last, aug_b, flat_high, flat_low, core, flat_sem, out_sem, core_sem):
+def fast_linear_kernel(cols, columns, early_ref, late_ref, lead_ref, inverse_ref, start_ref, high_ref, low_ref, factor_out, basis_out, core_ref, factor_ref, basis_ref, gram, split, work, aug_b, flat_high, flat_low, core, flat_sem, out_sem, core_sem, *augs):
     size, rank = start_ref.shape
     rows = size // 2
     width = core_ref.shape[2]
@@ -974,20 +1002,20 @@
         yield
         for step in range(per):
             at, below = step * BLOCK, (step + 1) * BLOCK
-            block = aug_f if below < rows else aug_last
-            load_augmented(block, work[at:below, at:below])
+            aug = augs[step]
+            for p in range(per - step):
+                aug[p] = work[at:below, at + p * BLOCK : below + p * BLOCK]
             for j in range(BLOCK // PANEL):
-                eliminate_panel(block, j)
+                eliminate_panel(aug, j)
                 yield
-            upper = jnp.where(row <= column, block[0], 0.0)
+            upper = jnp.where(row <= column, aug[0], 0.0)
             factor_ref[rows + at : rows + below, rows + at : rows + below] = upper.T
             if step > 0:
                 factor_ref[rows : rows + at, rows + at : rows + below] = jnp.zeros((at, BLOCK), jnp.float32)
             if below < rows:
-                left = six_terms(thirds(work[below:rows, at:below]), thirds(aug_f[1]), NT)
-                factor_ref[rows + below : size, rows + at : rows + below] = left
-                parts = thirds(left)
-                work[below:rows, below:rows] = work[below:rows, below:rows] - six_terms(parts, parts, NT)
+                across = jnp.concatenate([aug[p] for p in range(1, per - step)], axis=1)
+                factor_ref[rows + below : size, rows + at : rows + below] = across.T
+                work[below:rows, below:rows] = work[below:rows, below:rows] - self_product(thirds(across))
             yield
         loads[0].wait()
         leave(factor_ref.at[0:rows, :], factor_out.at[0:rows, :], out_sem.at[1])
@@ -1019,8 +1047,6 @@
             pltpu.VMEM((size, size), jnp.float32),
             pltpu.VMEM((3, size, size), jnp.bfloat16),
             pltpu.VMEM((rows, rows), jnp.float32),
-            pltpu.VMEM((2, BLOCK, BLOCK), jnp.float32),
-            pltpu.VMEM((1, BLOCK, BLOCK), jnp.float32),
             pltpu.VMEM((2, rank, rank), jnp.float32),
             pltpu.VMEM((size, width), jnp.bfloat16),
             pltpu.VMEM((size, width), jnp.bfloat16),
@@ -1028,6 +1054,7 @@
             pltpu.SemaphoreType.DMA((3,)),
             pltpu.SemaphoreType.DMA((4,)),
             pltpu.SemaphoreType.DMA((width // min(CHUNK, width),)),
+            *[pltpu.VMEM((rows // BLOCK - step, BLOCK, BLOCK), jnp.float32) for step in range(rows // BLOCK)],
         ],
         name="fast_linear",
     )(early, late, lead, inverse, start_basis, high, low)

time: 81.9 us -> 81.1 us (level)
  no operation moved by 1% of the time
where the time goes in v5:
time: 81.1 us; the launch traced here: 80.9 us
  Pallas kernels  80.1 us (99%)
    pallas_call x1, Pallas kernels, fast_gather(): pl.pallas_call(functools.partial(fast_gather_kernel, cols, columns), out_...  64.6 us
    pallas_call x1, Pallas kernels, fast_linear(): pl.pallas_call(functools.partial(fast_linear_kernel, lax.axis_size('col')...  15.5 us

profile of v5, /device:TPU:0, one launch (start us, length us, event | category | flops | bytes accessed | tf_op | source)
XLA Modules:
  0.0 80.9 jit_solution(4007053810026302207)
XLA Ops:
  0.6 64.6 %fast_gather.1 = (bf16[512,2048]{1,0:T(8,128)(2,1)}, bf16[512,2048]{1,0:T(8,128)(2,1)}, f32[1280,128]{1,0:T(8,128)}, f32[256,256]{1,0:T(8,128)}, f32[256,256]{1,0:T(8,128)}, /*index=5*/f32[512,128]{1,0:T(8,128)}) custom-call(f32[256,1,4096]{2,1,0:T(1,128)} %x_ref.1), custom_call_target="tpu_custom_call" | custom-call | tf_op jit(solution)/shard_map/fast_gather/pallas_call | solution.py:890
  65.2 15.5 %fast_linear.1 = (f32[512,512]{1,0:T(8,128)}, f32[512,128]{1,0:T(8,128)}, f32[128,1,2048]{2,1,0:T(1,128)}) custom-call(f32[1280,128]{1,0:T(8,128)} %get-tuple-element.9.early_ref, f32[512,128]{1,0:T(8,128)} %get-tuple-element.10.late_ref, f32[256,256]{1,0:T(8,128)} %get-tuple-element.11.lead_ref, f32[256,256]{1,0:T(8,128)} %get-tuple-element.12.inverse_ref, ...), custom_call_target="tpu_custom_call" | custom-call | tf_op jit(solution)/shard_map/fast_linear/pallas_call | solution.py:1035

commit v6 on v5

--- a/solution.py
+++ b/solution.py
@@ -531,7 +531,7 @@
 
 STRIPS = 8
 LATE = 4
-EARLY = 3
+EARLY = 4
 HELD = 3
 PIECES = STRIPS + 3
 
@@ -984,7 +984,7 @@
             load.wait()
         high, low = halves(basis)
         both = jnp.concatenate([high, low], axis=1)
-        piece = min(CHUNK, width)
+        piece = min(2 * CHUNK, width)
         for n, start in enumerate(range(0, width, piece)):
             part = slice(start, start + piece)
             product = contract(both, flat_high[:, part], TN)

time: 81.1 us -> 80.5 us (level)
  no operation moved by 1% of the time
where the time goes in v6:
time: 80.5 us; the launch traced here: 80.3 us
  Pallas kernels  79.5 us (99%)
    pallas_call x1, Pallas kernels, fast_gather(): pl.pallas_call(functools.partial(fast_gather_kernel, cols, columns), out_...  64.3 us
    pallas_call x1, Pallas kernels, fast_linear(): pl.pallas_call(functools.partial(fast_linear_kernel, lax.axis_size('col')...  15.3 us

profile of v6, /device:TPU:0, one launch (start us, length us, event | category | flops | bytes accessed | tf_op | source)
XLA Modules:
  0.0 80.3 jit_solution(7315531685699906131)
XLA Ops:
  0.6 64.3 %fast_gather.1 = (bf16[512,2048]{1,0:T(8,128)(2,1)}, bf16[512,2048]{1,0:T(8,128)(2,1)}, f32[1280,128]{1,0:T(8,128)}, f32[256,256]{1,0:T(8,128)}, f32[256,256]{1,0:T(8,128)}, /*index=5*/f32[512,128]{1,0:T(8,128)}) custom-call(f32[256,1,4096]{2,1,0:T(1,128)} %x_ref.1), custom_call_target="tpu_custom_call" | custom-call | tf_op jit(solution)/shard_map/fast_gather/pallas_call | solution.py:890
  64.9 15.3 %fast_linear.1 = (f32[512,512]{1,0:T(8,128)}, f32[512,128]{1,0:T(8,128)}, f32[128,1,2048]{2,1,0:T(1,128)}) custom-call(f32[1280,128]{1,0:T(8,128)} %get-tuple-element.9.early_ref, f32[512,128]{1,0:T(8,128)} %get-tuple-element.10.late_ref, f32[256,256]{1,0:T(8,128)} %get-tuple-element.11.lead_ref, f32[256,256]{1,0:T(8,128)} %get-tuple-element.12.inverse_ref, ...), custom_call_target="tpu_custom_call" | custom-call | tf_op jit(solution)/shard_map/fast_linear/pallas_call | solution.py:1035
